TPU v7x, 256 devices: a whole 4x4x8 slice. The times are simulated.
256 devices in a mesh: dp: 4 (over y_hi, core), expert: 64 (over x, z, y_lo).
Axes of the slice: x: 4, y: 4 (y_hi: 2, y_lo: 2; y = y_hi * 2 + y_lo), z: 8, core: 2. Of those that a mesh axis runs over, the one named last changes fastest.
Arguments:
- tokens: bfloat16 [4, 8192, 3584], P('dp', 'expert'), may hold values from -6 to 6
- cotangent: bfloat16 [4, 8192, 1024], P('dp', 'expert'), may hold values from -12 to 12
- gate_weights: float32 [4, 8192], replicated, may hold values from 0.1 to 1
- tile_expert: int32 [4, 64], replicated, may hold values from 0 to 63, as said below
- w_gate: bfloat16 [64, 3584, 1024], P('expert', None, 'dp'), may hold values from -0.09375 to 0.09375
- w_up: bfloat16 [64, 3584, 1024], P('expert', None, 'dp'), may hold values from -0.09375 to 0.09375
Outputs:
- d_tokens: bfloat16 [4, 8192, 3584], P('dp', 'expert')
- hidden: bfloat16 [4, 8192, 1024], P(None, 'expert', 'dp')
- grad_gate: bfloat16 [64, 3584, 1024], P('expert', None, 'dp')
- grad_up: bfloat16 [64, 3584, 1024], P('expert', None, 'dp')
Inputs may be any that keep to these rules, and one draw needn't show every extreme that they name: tile_expert[g, j] is either j or (j + 1) mod 64: the expert of the tile's own index of the expert axis or of the next index round the closed cycle.
All inputs are finite; a program needn't handle non-finite values.
Results may differ from a plain program's by a relative error of at most 0.009.
Values may be sent and summed in bfloat16 or wider, within the bound.
A program may use at most 128 MiB of HBM per device.

v0:
```python
import jax
import jax.numpy as jnp
from jax import lax
from jax.sharding import Mesh
from jax.sharding import PartitionSpec as P

TILE = 128
DP = ("dp_0", "dp_1")


def in_blocks(x, dim, count):
    before, after = (x.shape[:dim], x.shape[dim + 1 :])
    return jnp.moveaxis(x.reshape(*before, count, -1, *after), dim, 0)


def joined_along(pieces, dim):
    dims = list(pieces.shape[1:])
    dims[dim] *= pieces.shape[0]
    return jnp.moveaxis(pieces, 0, dim).reshape(dims)


def exchange_in_order(pieces, axes, order):
    inside = pieces.shape[1:]
    out = pieces.reshape(*(lax.axis_size(a) for a in axes), *inside)
    for k in order:
        out = lax.all_to_all(out, axes[k], k, k, tiled=True)
    return out.reshape(-1, *inside)


def core_and_chips(x, groups, order, split_dim, concat_dim):
    count = lax.axis_size(groups[0]) * lax.axis_size(groups[1])
    pieces = in_blocks(x, split_dim, count)
    return joined_along(exchange_in_order(pieces, groups, order), concat_dim)


def shifted(value, axis, steps):
    count = lax.axis_size(axis)
    pairs = [(source, (source + steps) % count) for source in range(count)]
    return lax.ppermute(value, axis, pairs)


def sent_and_summed(x, axis, dim):
    count = lax.axis_size(axis)
    pieces = lax.all_to_all(in_blocks(x, dim, count), axis, 0, 0, tiled=True)
    return jnp.sum(pieces.astype(jnp.float32), axis=0)


def contract(left, right, left_axis, right_axis):
    return lax.dot_general(
        left, right, (((left_axis,), (right_axis,)), ((), ())), preferred_element_type=jnp.float32
    )


def route_scale(tile_expert, gate_weights, source, expert, row_count):
    tile_count = row_count // TILE
    owners = lax.dynamic_slice_in_dim(tile_expert, source * tile_count, tile_count, 1)
    weights = lax.dynamic_slice_in_dim(gate_weights, source * row_count, row_count, 1)
    routed = jnp.repeat(owners == expert, TILE, axis=1, total_repeat_length=row_count)
    return jnp.where(routed, weights, jnp.zeros_like(weights))


def expert_pass(cand_rows, cand_grads, row_scale, gate_panel, up_panel):
    groups, row_total, model_width = cand_rows.shape
    quarter = gate_panel.shape[1]
    flat_rows = cand_rows.reshape(groups * row_total, model_width)
    gate_val = jnp.dot(flat_rows, gate_panel, preferred_element_type=jnp.float32)
    up_val = jnp.dot(flat_rows, up_panel, preferred_element_type=jnp.float32)
    sigmoid_val = jax.nn.sigmoid(gate_val)
    activation = gate_val * sigmoid_val
    factor = row_scale.reshape(groups * row_total, 1)
    hidden_part = (factor * activation * up_val).astype(jnp.bfloat16)
    act_grad = factor * cand_grads.reshape(groups * row_total, quarter).astype(jnp.float32)
    up_grad = (act_grad * activation).astype(jnp.bfloat16)
    gate_grad = (act_grad * up_val * sigmoid_val * (1.0 + gate_val * (1.0 - sigmoid_val))).astype(
        jnp.bfloat16
    )
    partial_value = (
        contract(gate_grad, gate_panel, 1, 1) + contract(up_grad, up_panel, 1, 1)
    ).astype(jnp.bfloat16)
    partial_value = lax.optimization_barrier(partial_value)
    grad_gate = contract(flat_rows, gate_grad, 0, 0)
    grad_up = contract(flat_rows, up_grad, 0, 0)
    return (
        partial_value.reshape(groups, row_total, model_width),
        hidden_part.reshape(groups, row_total, quarter),
        grad_gate,
        grad_up,
    )


def to_groups(tile_rows, tile_grads):
    gathered = lax.all_gather(tile_rows, DP, axis=0, tiled=True)
    quarters = core_and_chips(tile_grads, ("dp_0", "dp_1"), (1, 0), 2, 0)
    return (gathered, quarters)


def cycle_ahead(tile_rows, tile_grads):
    return shifted((tile_rows, tile_grads), "expert", 1)


def cycle_return(row_sums, hidden_part):
    return shifted((row_sums, hidden_part), "expert", -1)


def quarter_total(terms):
    return sent_and_summed(terms.astype(jnp.bfloat16), DP, 0)


def per_device(tokens, cotangent, gate_weights, tile_expert, w_gate, w_up):
    row_count = tokens.shape[1]
    cycle_size = lax.axis_size("expert")
    position = lax.axis_index("expert")
    prev_place = (position + cycle_size - 1) % cycle_size
    gate_panel = w_gate[0]
    up_panel = w_up[0]
    own_scale = route_scale(tile_expert, gate_weights, position, position, row_count)
    prev_scale = route_scale(tile_expert, gate_weights, prev_place, position, row_count)
    near_rows, near_grads = cycle_ahead(tokens, cotangent)
    cand_rows, cand_grads = to_groups(
        jnp.concatenate([tokens, near_rows], 1), jnp.concatenate([cotangent, near_grads], 1)
    )
    row_scale = jnp.concatenate([own_scale, prev_scale], 1)
    partial_value, hidden_part, grad_gate, grad_up = expert_pass(
        cand_rows, cand_grads, row_scale, gate_panel, up_panel
    )
    summed = quarter_total(partial_value.astype(jnp.float32)).astype(jnp.bfloat16)
    back_rows, back_hidden = cycle_return(summed[:, row_count:], hidden_part[:, row_count:])
    d_tokens = (summed[:, :row_count].astype(jnp.float32) + back_rows.astype(jnp.float32)).astype(
        jnp.bfloat16
    )
    hidden = (
        hidden_part[:, :row_count].astype(jnp.float32) + back_hidden.astype(jnp.float32)
    ).astype(jnp.bfloat16)
    grad_gate = (grad_gate / TILE).astype(jnp.bfloat16)[None]
    grad_up = (grad_up / TILE).astype(jnp.bfloat16)[None]
    return (d_tokens, hidden, grad_gate, grad_up)


def solution(mesh):
    split = Mesh(mesh.devices.reshape(2, 2, mesh.shape["expert"]), ("dp_0", "dp_1", "expert"))
    placed = (
        P(DP, "expert", None),
        P(DP, "expert", None),
        P(),
        P(),
        P("expert", None, DP),
        P("expert", None, DP),
    )
    return jax.shard_map(
        per_device,
        mesh=split,
        in_specs=placed,
        out_specs=(
            P(DP, "expert", None),
            P(None, "expert", DP),
            P("expert", None, DP),
            P("expert", None, DP),
        ),
        check_vma=False,
    )
```

profile of v0, /device:TPU:1, one launch (start us, length us, event | category | flops | bytes accessed | tf_op | source)
XLA Modules:
  0.0 264.1 jit_solution(17189211925136848051)
XLA Ops:
  7.2 0.0 copy-start
  7.2 0.0 copy-start.4
  7.2 0.0 copy-start.5
  7.2 0.0 all-gather.2.cloned.1.call-start
  7.2 2.2 collective-permute-start.1
  9.4 27.8 %collective-permute-done.1 = bf16[1,128,3584]{2,1,0:T(8,128)(2,1)S(1)} collective-permute-done((bf16[1,128,3584]{2,1,0:T(8,128)(2,1)}, bf16[1,128,3584]{2,1,0:T(8,128)(2,1)S(1)}, u32[]{:S(2)}, u32[]{:S(2)}) %collective-permute-start.1) | collective-permute-done | bytes 917536 | tf_op jit(solution)/shard_map/ppermute | solution.py:39
  37.2 2.5 pad_maximum_fusion
  39.7 0.0 all-gather.2.cloned.1.call-update
  39.7 0.0 copy-done.4
  39.7 0.2 copy.17
  39.9 0.1 collective-permute-start
  40.0 0.0 copy-done.5
  40.0 0.2 fusion.18
  40.3 0.8 dynamic-slice_select_fusion.1
  41.1 9.8 %collective-permute-done = bf16[1,128,1024]{1,2,0:T(8,128)(2,1)S(1)} collective-permute-done((bf16[1,128,1024]{1,2,0:T(8,128)(2,1)S(1)}, bf16[1,128,1024]{1,2,0:T(8,128)(2,1)S(1)}, u32[]{:S(2)}, u32[]{:S(2)}) %collective-permute-start) | collective-permute-done | bytes 262176 | tf_op jit(solution)/shard_map/ppermute | solution.py:39
  50.8 0.1 pad_maximum_fusion.1
  50.9 0.2 copy.19
  51.1 6.1 %all_to_all.15 = bf16[2,2,1,256,256]{4,3,0,2,1:T(8,128)(2,1)S(1)} all-to-all(bf16[2,2,1,256,256]{4,3,0,2,1:T(8,128)(2,1)S(1)} %copy.19), channel_id=1, replica_groups=mesh['dp_0'=2,'dp_1'=2,'expert'=64] {'dp_1'}, dimensions={1} | all-to-all | bytes 1048576 | tf_op jit(solution)/shard_map/all_to_all | solution.py:26
  57.3 0.8 copy.20
  58.1 3.9 %all-to-all-start.1 = ((bf16[2,2,1,256,256]{4,3,1,2,0:T(8,128)(2,1)}), bf16[2,2,1,256,256]{4,3,1,2,0:T(8,128)(2,1)S(1)}, u32[]{:S(2)}, u32[]{:S(2)}) async-start(bf16[2,2,1,256,256]{4,3,1,2,0:T(8,128)(2,1)} %copy.20), calls=%async_computation.1 | async-start | bytes 1048576 | tf_op jit(solution)/shard_map/all_to_all | solution.py:26
  62.0 41.2 %all-gather.2.cloned.1.call-done = bf16[4,256,3584]{2,1,0:T(8,128)(2,1)} async-done(((bf16[1,256,3584]{2,1,0:T(8,128)(2,1)}), bf16[4,256,3584]{2,1,0:T(8,128)(2,1)}) %all-gather.2.cloned.1.call-update) | async-done | bytes 7340048 | tf_op jit(solution)/shard_map/all_gather | solution.py:92
  103.2 6.6 %fusion.6 = f32[1024,256]{1,0:T(8,128)} fusion(bf16[1024,3584]{1,0:T(8,128)(2,1)} %bitcast.49, bf16[1,3584,256]{2,1,0:T(8,128)(2,1)} %param.20), kind=kOutput, calls=%fused_computation.10 | convolution fusion | flops 1879048192 | bytes 10223616 | tf_op jit(solution)/shard_map/dot_general | solution.py:66
  109.8 0.0 all-to-all-done.1
  109.8 0.0 copy-start.3
  109.8 0.8 copy-done.3
  110.6 0.0 copy-done
  110.6 0.0 copy-start.2
  110.6 5.9 %multiply_convert_fusion = (bf16[1024,256]{1,0:T(8,128)(2,1)S(1)}, bf16[1024,256]{1,0:T(8,128)(2,1)S(1)}, bf16[1024,256]{1,0:T(8,128)(2,1)S(1)}) fusion(f32[1024]{0:T(1024)S(1)} %bitcast.48, f32[1024,256]{1,0:T(8,128)} %fusion.6, bf16[2,2,1,256,256]{4,3,1,2,0:T(8,128)(2,1)} %copy-done.3, bf16[1024,3584]{1,0:T(8,128)(2,1)} %bitcast.50, ...), kind=kOutput, calls=%fused_computation.23 | convolution fusion | flops 1883766784 | bytes 12324864 | tf_op jit(solution)/shard_map/dot_general | solution.py:67
  116.5 0.0 copy-done.2
  116.5 7.3 %fusion.4 = f32[1024,3584]{1,0:T(8,128)} fusion(bf16[1024,256]{1,0:T(8,128)(2,1)S(1)} %get-tuple-element.48, bf16[1,3584,256]{2,1,0:T(8,128)(2,1)S(1)} %copy-done.2), kind=kOutput, calls=%fused_computation.8 | convolution fusion | flops 1879048192 | bytes 17039360 | tf_op jit(solution)/shard_map/dot_general | solution.py:49
  123.9 10.2 %add_convert_fusion = bf16[1024,3584]{1,0:T(8,128)(2,1)} fusion(f32[1024,3584]{1,0:T(8,128)} %fusion.4, bf16[1024,256]{1,0:T(8,128)(2,1)S(1)} %get-tuple-element.49, bf16[1,3584,256]{2,1,0:T(8,128)(2,1)S(1)} %copy-done), kind=kOutput, calls=%fused_computation | convolution fusion | flops 1886388224 | bytes 24379392 | tf_op jit(solution)/shard_map/dot_general | solution.py:49
  134.1 5.7 %all-to-all-start.2 = ((bf16[4,1,256,3584]{3,2,1,0:T(8,128)(2,1)}), bf16[4,1,256,3584]{3,2,1,0:T(8,128)(2,1)}, u32[]{:S(2)}, u32[]{:S(2)}) async-start(bf16[4,1,256,3584]{3,2,1,0:T(8,128)(2,1)} %bitcast.42), calls=%async_computation.2 | async-start | bytes 14680064 | tf_op jit(solution)/shard_map/all_to_all | solution.py:44
  139.8 0.7 slice.47
  140.5 5.2 %collective-permute-start.3 = (bf16[4,128,256]{2,1,0:T(8,128)(2,1)}, bf16[4,128,256]{2,1,0:T(8,128)(2,1)}, u32[]{:S(2)}, u32[]{:S(2)}) collective-permute-start(bf16[4,128,256]{2,1,0:T(8,128)(2,1)} %slice.47), channel_id=1, source_target_pairs={{0,63},{1,0},{2,1},{3,2},{4,3},{5,4},{6,5},{7,6},{8,7},{9,8},{10,9... | collective-permute-start | bytes 786440 | tf_op jit(solution)/shard_map/ppermute | solution.py:39
  145.7 6.4 %fusion.3 = bf16[1,3584,256]{2,1,0:T(8,128)(2,1)} fusion(bf16[1024,3584]{1,0:T(8,128)(2,1)} %bitcast.51, bf16[1024,256]{1,0:T(8,128)(2,1)S(1)} %get-tuple-element.48), kind=kOutput, calls=%fused_computation.6 | convolution fusion | flops 1880883200 | bytes 9699328 | tf_op jit(solution)/shard_map/dot_general | solution.py:49
  152.1 75.8 %all-to-all-done.2 = bf16[4,1,256,3584]{3,2,1,0:T(8,128)(2,1)} async-done(((bf16[4,1,256,3584]{3,2,1,0:T(8,128)(2,1)}), bf16[4,1,256,3584]{3,2,1,0:T(8,128)(2,1)}, u32[]{:S(2)}, u32[]{:S(2)}) %all-to-all-start.2) | async-done | bytes 7340064 | tf_op jit(solution)/shard_map/all_to_all | solution.py:44
  227.9 6.0 %reduce_sum.14 = bf16[256,3584]{1,0:T(8,128)(2,1)} reduce(bf16[4,1,256,3584]{3,2,1,0:T(8,128)(2,1)} %all-to-all-done.2, bf16[]{:T(256)} %constant.151.clone.1), dimensions={0,1}, to_apply=%region_0.2 | reduce | flops 2752512 | bytes 9175042 | tf_op jit(solution)/shard_map/reduce_sum | solution.py:45
  233.9 1.2 slice.45
  235.1 0.0 copy-start.1
  235.1 0.1 collective-permute-start.2
  235.2 6.6 %fusion.2 = bf16[1,3584,256]{2,1,0:T(8,128)(2,1)} fusion(bf16[1024,3584]{1,0:T(8,128)(2,1)} %bitcast.52, bf16[1024,256]{1,0:T(8,128)(2,1)S(1)} %get-tuple-element.49), kind=kOutput, calls=%fused_computation.5 | convolution fusion | flops 1880883200 | bytes 9699328 | tf_op jit(solution)/shard_map/dot_general | solution.py:49
  241.8 0.0 collective-permute-done.3
  241.8 1.7 add_convert_fusion.2
  243.5 12.6 %collective-permute-done.2 = bf16[1,128,3584]{2,1,0:T(8,128)(2,1)S(1)} collective-permute-done((bf16[1,128,3584]{2,1,0:T(8,128)(2,1)S(1)}, bf16[1,128,3584]{2,1,0:T(8,128)(2,1)S(1)}, u32[]{:S(2)}, u32[]{:S(2)}) %collective-permute-start.2) | collective-permute-done | bytes 917536 | tf_op jit(solution)/shard_map/ppermute | solution.py:39
  256.1 0.0 copy-done.1
  256.1 1.1 add_convert_fusion.1
  (2 shorter events, 0.0 us)
Async XLA Ops:
  7.2 103.4 %copy-start = (bf16[1,3584,256]{2,1,0:T(8,128)(2,1)S(1)}, bf16[1,3584,256]{2,1,0:T(8,128)(2,1)}, u32[]{:S(2)}) copy-start(bf16[1,3584,256]{2,1,0:T(8,128)(2,1)} %param.21) | copy-start | bytes 5505028
  7.2 32.6 %copy-start.4 = (bf16[1,128,1024]{2,1,0:T(8,128)(2,1)S(1)}, bf16[1,128,1024]{2,1,0:T(8,128)(2,1)}, u32[]{:S(2)}) copy-start(bf16[1,128,1024]{2,1,0:T(8,128)(2,1)} %param.17) | copy-start | bytes 786436
  7.2 32.8 %copy-start.5 = (s32[4,64]{1,0:T(4,128)S(1)}, s32[4,64]{1,0:T(4,128)}, u32[]{:S(2)}) copy-start(s32[4,64]{1,0:T(4,128)} %param.19) | copy-start | bytes 3076
  7.2 96.0 %all-gather.2.cloned.1.call-start = ((), (), s32[]{:S(2)}) async-start(), calls=%async_computation.3 | async-start | bytes 9175040 | tf_op jit(solution)/shard_map/all_gather | solution.py:92
  7.2 29.9 %collective-permute-start.1 = (bf16[1,128,3584]{2,1,0:T(8,128)(2,1)}, bf16[1,128,3584]{2,1,0:T(8,128)(2,1)S(1)}, u32[]{:S(2)}, u32[]{:S(2)}) collective-permute-start(bf16[1,128,3584]{2,1,0:T(8,128)(2,1)} %param.16), channel_id=1, source_target_pairs={{0,1},{1,2},{2,3},{3,4},{4,5},{5,6},{6,7},{7,8},{8,9},{9,10},{10,1... | collective-permute-start | bytes 2752520 | tf_op jit(solution)/shard_map/ppermute | solution.py:39
  39.9 10.9 %collective-permute-start = (bf16[1,128,1024]{1,2,0:T(8,128)(2,1)S(1)}, bf16[1,128,1024]{1,2,0:T(8,128)(2,1)S(1)}, u32[]{:S(2)}, u32[]{:S(2)}) collective-permute-start(bf16[1,128,1024]{1,2,0:T(8,128)(2,1)S(1)} %copy.17), channel_id=1, source_target_pairs={{0,1},{1,2},{2,3},{3,4},{4,5},{5,6},{6,7},{7,8},{8,9},{9,10},{10,1... | collective-permute-start | bytes 786440 | tf_op jit(solution)/shard_map/ppermute | solution.py:39
  58.1 51.7 %all-to-all-start.1 = ((bf16[2,2,1,256,256]{4,3,1,2,0:T(8,128)(2,1)}), bf16[2,2,1,256,256]{4,3,1,2,0:T(8,128)(2,1)S(1)}, u32[]{:S(2)}, u32[]{:S(2)}) async-start(bf16[2,2,1,256,256]{4,3,1,2,0:T(8,128)(2,1)} %copy.20), calls=%async_computation.1 | async-start | bytes 1048576 | tf_op jit(solution)/shard_map/all_to_all | solution.py:26
  109.8 0.8 copy-start.3
  110.6 5.9 %copy-start.2 = (bf16[1,3584,256]{2,1,0:T(8,128)(2,1)S(1)}, bf16[1,3584,256]{2,1,0:T(8,128)(2,1)}, u32[]{:S(2)}) copy-start(bf16[1,3584,256]{2,1,0:T(8,128)(2,1)} %param.20) | copy-start | bytes 5505028
  134.1 93.8 %all-to-all-start.2 = ((bf16[4,1,256,3584]{3,2,1,0:T(8,128)(2,1)}), bf16[4,1,256,3584]{3,2,1,0:T(8,128)(2,1)}, u32[]{:S(2)}, u32[]{:S(2)}) async-start(bf16[4,1,256,3584]{3,2,1,0:T(8,128)(2,1)} %bitcast.42), calls=%async_computation.2 | async-start | bytes 14680064 | tf_op jit(solution)/shard_map/all_to_all | solution.py:44
  140.5 101.3 %collective-permute-start.3 = (bf16[4,128,256]{2,1,0:T(8,128)(2,1)}, bf16[4,128,256]{2,1,0:T(8,128)(2,1)}, u32[]{:S(2)}, u32[]{:S(2)}) collective-permute-start(bf16[4,128,256]{2,1,0:T(8,128)(2,1)} %slice.47), channel_id=1, source_target_pairs={{0,63},{1,0},{2,1},{3,2},{4,3},{5,4},{6,5},{7,6},{8,7},{9,8},{10,9... | collective-permute-start | bytes 786440 | tf_op jit(solution)/shard_map/ppermute | solution.py:39
  235.1 21.0 %copy-start.1 = (bf16[256,3584]{1,0:T(8,128)(2,1)S(1)}, bf16[256,3584]{1,0:T(8,128)(2,1)}, u32[]{:S(2)}) copy-start(bf16[256,3584]{1,0:T(8,128)(2,1)} %reduce_sum.14) | copy-start | bytes 5505028
  235.1 21.0 %collective-permute-start.2 = (bf16[1,128,3584]{2,1,0:T(8,128)(2,1)S(1)}, bf16[1,128,3584]{2,1,0:T(8,128)(2,1)S(1)}, u32[]{:S(2)}, u32[]{:S(2)}) collective-permute-start(bf16[1,128,3584]{2,1,0:T(8,128)(2,1)S(1)} %slice.45), channel_id=1, source_target_pairs={{0,63},{1,0},{2,1},{3,2},{4,3},{5,4},{6,5},{7,6},{8,7},{9,8},{10,9... | collective-permute-start | bytes 2752520 | tf_op jit(solution)/shard_map/ppermute | solution.py:39
Sparse Core Ops, SparseCore 0:
  39.9 63.2 all-gather.1
where the time goes:
time: 265 us; the launch traced here: 264 us
  waiting for transfers between devices  167 us (63%)
  matrix products  43.1 us (16%)
  starting transfers between devices  17.1 us (6%)
  between operations  14.2 us (5%)
  other arithmetic  12.4 us (5%)
  blocking collectives  6.15 us (2%)
  local copies, waits for them, and re-layouts  3.98 us (2%)
    all_to_all x1, waiting for transfers between devices, sent_and_summed(): pieces = lax.all_to_all(in_blocks(x, dim, count), axis, 0, 0, tiled=True)  75.8 us
    ppermute x4, waiting for transfers between devices, shifted(): return lax.ppermute(value, axis, pairs)  50.2 us
    all_gather x1, waiting for transfers between devices, to_groups(): gathered = lax.all_gather(tile_rows, DP, axis=0, tiled=True)  41.2 us
    dot_general x4, matrix products, contract(): lax.dot_general(left, right, (((left_axis,), (right_axis,)), ((), ())), p...  30.5 us
    ppermute x4, starting transfers between devices, shifted(): return lax.ppermute(value, axis, pairs)  7.54 us
    dot_general x1, matrix products, expert_pass(): jnp.dot(flat_rows, gate_panel, preferred_element_type=jnp.float32)  6.61 us
    all_to_all x1, blocking collectives, exchange_in_order(): out = lax.all_to_all(out, axes[k], k, k, tiled=True)  6.15 us
    reduce_sum x1, other arithmetic, sent_and_summed(): return jnp.sum(pieces.astype(jnp.float32), axis=0)  6.01 us
  transfers between devices with their start and end apart: 7, of which 5 were waited for; matrix products, arithmetic and copies ran while one was open for 12% of the time, Pallas kernels for 0%

commit v1 on v0

v1 whole, which is shorter than its diff:
```python
import functools

import jax
import jax.numpy as jnp
from jax import lax
from jax.experimental import pallas as pl
from jax.experimental.pallas import tpu as pltpu
from jax.sharding import PartitionSpec as P

MESH = pl.DeviceIdType.MESH
F32 = jnp.float32
BF16 = jnp.bfloat16
K = 4
N_COLS = 512


def dot_nn(a, b):
    return lax.dot_general(a, b, (((1,), (0,)), ((), ())), preferred_element_type=F32)


def dot_nt(a, b):
    return lax.dot_general(a, b, (((1,), (1,)), ((), ())), preferred_element_type=F32)


def dot_tn(a, b):
    return lax.dot_general(a, b, (((0,), (0,)), ((), ())), preferred_element_type=F32)


def kernel(
    experts,
    tok, cot, gw, te, wg_hbm, wu_hbm,
    dtok, hid, ggrad, ugrad,
    xr, ch, cs, gwv, wg, wu, gu, hv, hb, po, ps, sp, mv, zc, fin, wgo, wuo,
    s_ring, r_ring, s_opp, r_opp, s_z, r_z, s_sib, r_sib,
    s_cot, r_cot, s_ps, r_ps, s_m, r_m, s_zc, r_zc, s_fin, r_fin, s_hid, r_hid,
    l_in, l_gw, l_hid, l_wg, l_dt,
):
    tile = tok.shape[1]
    width = tok.shape[2]
    quarter = wg_hbm.shape[2]
    half = 2 * quarter
    rows = tile // K
    d = lax.axis_index("dp")
    e = lax.axis_index("expert")
    hi, c = d // 2, d % 2
    lo = e % 2
    prev = (e + experts - 1) % experts

    y_e = e + 1 - 2 * lo
    yp = ((d + 2 * lo) % 4, y_e)
    ym = ((d + 2 * (1 - lo)) % 4, y_e)
    sib = (d + 1 - 2 * c, e)
    zn = (d, (e + 2) % experts)
    zp = (d, (e + experts - 2) % experts)
    nxt = (d, (e + 1) % experts)
    prv = (d, prev)

    def remote(src, dst, send, recv, dev):
        return pltpu.make_async_remote_copy(
            src_ref=src, dst_ref=dst, send_sem=send, recv_sem=recv, device_id=dev, device_id_type=MESH
        )

    def arrived(dst, recv):
        remote(dst, dst, s_m.at[0], recv, sib).wait_recv()

    def sent(src, send):
        remote(src, src, send, r_m.at[0], sib).wait_send()

    def chunk(k, base=0, count=1):
        return pl.ds(base + k * rows, rows * count)

    even = lo == 0
    odd = lo == 1

    own_x = pltpu.make_async_copy(tok.at[0], xr.at[0, pl.ds(0, tile)], l_in.at[0])
    own_c = pltpu.make_async_copy(
        cot.at[0, :, pl.ds(pl.multiple_of(hi * half, half), half)], ch.at[0], l_in.at[1]
    )
    load_g = pltpu.make_async_copy(wg_hbm.at[0], wg, l_in.at[2])
    load_u = pltpu.make_async_copy(wu_hbm.at[0], wu, l_in.at[3])
    gw_own = pltpu.make_async_copy(gw.at[:, pl.ds(pl.multiple_of(e * tile, tile), tile)], gwv.at[0], l_gw.at[0])
    gw_prev = pltpu.make_async_copy(
        gw.at[:, pl.ds(pl.multiple_of(prev * tile, tile), tile)], gwv.at[1], l_gw.at[1]
    )
    own_x.start()
    own_c.start()
    load_g.start()
    load_u.start()
    gw_own.start()
    gw_prev.start()

    barrier = pltpu.get_barrier_semaphore()
    for dev in (yp, ym, sib):
        pl.semaphore_signal(barrier, inc=1, device_id=dev, device_id_type=MESH)

    @pl.when(even)
    def _():
        pl.semaphore_signal(barrier, inc=1, device_id=zn, device_id_type=MESH)
        pl.semaphore_signal(barrier, inc=1, device_id=zp, device_id_type=MESH)
        pl.semaphore_wait(barrier, 6)

    @pl.when(odd)
    def _():
        pl.semaphore_signal(barrier, inc=1, device_id=nxt, device_id_type=MESH)
        pl.semaphore_wait(barrier, 3)

    to1 = (1 + 3 * lo, 0)
    to3 = (3 + lo, tile * lo)
    at1 = (4 - 3 * lo, 0)
    at3 = (4 - lo, tile * (1 - lo))

    def ring1(k, src, slot, base):
        return remote(src, xr.at[slot, chunk(k, base)], s_ring.at[k], r_ring.at[k], yp)

    def ring3(k, src, slot, base):
        return remote(src, xr.at[slot, chunk(k, base)], s_ring.at[K + k], r_ring.at[K + k], ym)

    h_yp = lax.rem(hi + lo, 2)
    h_ym = lax.rem(hi + 1 - lo, 2)
    cot1 = remote(
        cot.at[0, :, pl.ds(pl.multiple_of(h_yp * half, half), half)], ch.at[1 + 3 * lo], s_cot.at[0], r_cot.at[0], yp
    )
    cot3 = remote(
        cot.at[0, :, pl.ds(pl.multiple_of(h_ym * half, half), half)], ch.at[3 + 2 * lo], s_cot.at[1], r_cot.at[1], ym
    )

    for k in range(K):
        ring1(k, tok.at[0, chunk(k)], *to1).start()
        ring3(K - 1 - k, tok.at[0, chunk(K - 1 - k)], *to3).start()
        if k == 0:
            cot1.start()
            cot3.start()

    mine = pl.ds(pl.multiple_of(c * quarter, quarter), quarter)
    other = pl.ds(pl.multiple_of((1 - c) * quarter, quarter), quarter)

    def sib_x(s):
        return remote(xr.at[s, pl.ds(0, tile)], xr.at[s, pl.ds(tile, tile)], s_sib.at[s], r_sib.at[s], sib)

    def sib_c(s):
        return remote(ch.at[s, :, other], cs.at[s], s_cot.at[5 + s], r_cot.at[5 + s], sib)

    def to_sibling(s):
        sib_x(s).start()
        sib_c(s).start()

    def from_sibling(s):
        sib_x(s).wait_recv()
        sib_c(s).wait_recv()

    own_x.wait()
    own_c.wait()
    to_sibling(0)

    eye = lax.broadcasted_iota(jnp.int32, (tile, tile), 0) == lax.broadcasted_iota(jnp.int32, (tile, tile), 1)
    gw_own.wait()
    gw_prev.wait()

    def scale_of(group, place, which):
        line = gwv[which, pl.ds(group, 1), :]
        routed = jnp.where(te[group, place] == e, jnp.float32(1.0), jnp.float32(0.0))
        spread = jnp.where(eye, jnp.broadcast_to(line, (tile, tile)), jnp.float32(0.0))
        return jnp.sum(spread, axis=1, keepdims=True) * routed

    def group_half(s):
        return (hi, (hi + 1 - lo) % 2, 1 - hi, (hi + lo) % 2)[s]

    def forward(s, dyn):
        gh, place, which = s
        x = xr[dyn]
        gate = dot_nn(x, wg[...])
        up = dot_nn(x, wu[...])
        for part in range(2):
            group = gh * 2 + (c if part == 0 else 1 - c)
            w = scale_of(group, place, which)
            r = slice(part * tile, (part + 1) * tile)
            dh = (ch[dyn, :, mine] if part == 0 else cs[dyn]).astype(F32)
            g, u = gate[r], up[r]
            sg = jax.nn.sigmoid(g)
            act = g * sg
            hv[dyn, r, :] = ((w * act) * u).astype(BF16)
            ag = w * dh
            gu[dyn, r, 0:quarter] = (ag * u * sg * (1.0 + g * (1.0 - sg))).astype(BF16)
            gu[dyn, r, quarter:half] = (ag * act).astype(BF16)

    def input_grad(dyn):
        gg = gu[dyn, :, 0:quarter]
        ug = gu[dyn, :, quarter:half]

        @pl.loop(0, width // N_COLS)
        def _(n):
            cols = pl.ds(pl.multiple_of(n * N_COLS, N_COLS), N_COLS)
            part = dot_nt(gg, wg[cols, :]) + dot_nt(ug, wu[cols, :])
            po[dyn, :, cols] = part[0:tile].astype(BF16)
            ps[dyn, :, cols] = part[tile:].astype(BF16)

    def sib_ps(s):
        return remote(ps.at[s], sp.at[s], s_ps.at[s], r_ps.at[s], sib)

    def add_rows(dst_slot, src):
        @pl.loop(0, K)
        def _(k):
            r = pl.ds(pl.multiple_of(k * rows, rows), rows)
            po[dst_slot, r, :] = (po[dst_slot, r, :].astype(F32) + src[r, :].astype(F32)).astype(BF16)

    load_g.wait()
    load_u.wait()
    from_sibling(0)
    forward((hi, e, 0), 0)

    def got1(k):
        slot, base = at1
        arrived(xr.at[slot, chunk(k, base)], r_ring.at[k])

    def got3(k):
        slot, base = at3
        arrived(xr.at[slot, chunk(k, base)], r_ring.at[K + k])

    def z1(k):
        return remote(xr.at[4, chunk(k)], xr.at[1, chunk(k)], s_z.at[k], r_z.at[k], zn)

    def z3(k):
        return remote(xr.at[4, chunk(k, tile)], xr.at[3, chunk(k)], s_z.at[K + k], r_z.at[K + k], zn)

    def opp1(k):
        slot, base = at1
        return remote(xr.at[slot, chunk(k, base)], xr.at[2, chunk(k)], s_opp.at[k], r_opp.at[k], yp)

    def opp3(k):
        slot, base = at3
        return remote(xr.at[slot, chunk(k, base)], xr.at[2, chunk(k)], s_opp.at[k], r_opp.at[k], ym)

    arrived(ch.at[4 - 3 * lo], r_cot.at[0])
    arrived(ch.at[5 - 2 * lo], r_cot.at[1])
    relay_dev = ((d + 2 * lo + 2 * lo) % 4, y_e)
    relay_dev = (lax.rem(d + 4 * lo, 4), y_e)
    cot_opp = remote(ch.at[4 - lo], ch.at[2], s_cot.at[2], r_cot.at[2], relay_dev)
    cot_opp.start()
    cot_z1 = remote(ch.at[4], ch.at[1], s_cot.at[3], r_cot.at[3], zn)
    cot_z3 = remote(ch.at[5], ch.at[3], s_cot.at[4], r_cot.at[4], zn)

    @pl.when(even)
    def _():
        cot_z1.start()
        cot_z3.start()

    got1(0)
    got3(K - 1)

    @pl.when(even)
    def _():
        z1(0).start()

    opp1(0).start()
    opp3(K - 1).start()
    input_grad(0)
    sib_ps(0).start()

    for k in range(1, K):
        got1(k)
        got3(K - 1 - k)

        @pl.when(even)
        def _():
            z1(k).start()

        if k < K // 2:
            opp1(k).start()
            opp3(K - 1 - k).start()

    @pl.when(even)
    def _():
        for k in range(K):
            z3(K - 1 - k).start()

    sib_ps(0).wait_recv()
    add_rows(0, sp.at[0])

    @pl.when(odd)
    def _():
        to_sibling(1)
        to_sibling(3)

    @pl.when(even)
    def _():
        cot_z1.wait_recv()
        for k in range(K):
            z1(k).wait_recv()
        to_sibling(1)

    from_sibling(1)
    forward((group_half(1), prev, 1), 1)
    input_grad(1)
    sib_ps(1).start()

    def zq(j, k):
        return remote(po.at[1 + 2 * j, chunk(k)], zc.at[j, chunk(k)], s_zc.at[K * j + k], r_zc.at[K * j + k], zp)

    def fin_of(j, k, src):
        return remote(src, fin.at[j, chunk(k)], s_fin.at[K * j + k], r_fin.at[K * j + k], ym if j == 0 else yp)

    def hid_of(j):
        dst = (1 - lo) if j == 0 else lo
        return remote(hv.at[1 + 2 * j], hb.at[dst], s_hid.at[j], r_hid.at[dst], prv)

    hid_of(0).start()

    third = 2 + lo
    fourth = 3 - lo

    @pl.when(even)
    def _():
        for k in range(K):
            arrived(xr.at[2, chunk(k)], r_opp.at[k])
        cot_opp.wait_recv()
        to_sibling(2)

    def dyn_from_sibling(s):
        arrived(xr.at[s, pl.ds(tile, tile)], r_sib.at[s])
        arrived(cs.at[s], r_cot.at[5 + s])

    sib_ps(1).wait_recv()
    add_rows(1, sp.at[1])

    @pl.when(even)
    def _():
        for k in range(K):
            zq(0, k).start()

    @pl.when(odd)
    def _():
        for k in range(K // 2, K):
            fin_of(0, k, po.at[1, chunk(k)]).start()

    dyn_from_sibling(third)
    gh_opp = 1 - hi
    gh_three = group_half(3)
    forward(
        (gh_opp * (1 - lo) + gh_three * lo, e * (1 - lo) + prev * lo, lo),
        third,
    )
    input_grad(third)

    def dyn_ps(s):
        return remote(ps.at[s], sp.at[s], s_ps.at[s], r_ps.at[s], sib)

    dyn_ps(third).start()

    @pl.when(odd)
    def _():
        hid_of(1).start()
        for k in range(K):
            arrived(xr.at[2, chunk(k)], r_opp.at[k])
        cot_opp.wait_recv()
        to_sibling(2)

    dyn_ps(third).wait_recv()
    add_rows(third, sp.at[third])

    hk = K // 2

    def m_of(j):
        r = chunk(j * hk, 0, hk)
        return remote(po.at[2, r], mv.at[j], s_m.at[j], r_m.at[j], ym if j == 0 else yp)

    @pl.when(even)
    def _():
        m_of(0).start()
        m_of(1).start()
        cot_z3.wait_recv()
        for k in range(K):
            z3(k).wait_recv()
        to_sibling(3)

    @pl.when(odd)
    def _():
        for k in range(hk):
            fin_of(1, k, po.at[3, chunk(k)]).start()

    dyn_from_sibling(fourth)
    forward(
        (gh_opp * lo + gh_three * (1 - lo), e * lo + prev * (1 - lo), 1 - lo),
        fourth,
    )
    input_grad(fourth)
    dyn_ps(fourth).start()

    @pl.when(even)
    def _():
        hid_of(1).start()

    dyn_ps(fourth).wait_recv()
    add_rows(fourth, sp.at[fourth])

    @pl.when(even)
    def _():
        for k in range(K):
            zq(1, k).start()

    @pl.when(odd)
    def _():
        m_of(0).start()
        m_of(1).start()

    m_of(0).wait_recv()
    m_of(1).wait_recv()

    def merge(dst, r, m_rows, m_slot):
        dst[r, :] = (dst[r, :].astype(F32) + mv[m_slot, m_rows, :].astype(F32)).astype(BF16)

    @pl.when(odd)
    def _():
        for k in range(hk):
            merge(po.at[1], chunk(k), chunk(k), 0)
            fin_of(0, k, po.at[1, chunk(k)]).start()
        for k in range(hk, K):
            merge(po.at[3], chunk(k), chunk(k - hk), 1)
            fin_of(1, k, po.at[3, chunk(k)]).start()

    @pl.when(even)
    def _():
        for k in range(K):
            zq(0, k).wait_recv()
            if k < hk:
                merge(zc.at[0], chunk(k), chunk(k), 0)
            fin_of(0, k, zc.at[0, chunk(k)]).start()

    @pl.loop(0, width // N_COLS)
    def _(n):
        cols = pl.ds(pl.multiple_of(n * N_COLS, N_COLS), N_COLS)
        x = xr[0:4, :, cols].reshape(8 * tile, N_COLS)
        grads = gu[...].reshape(8 * tile, half)
        total = dot_tn(x, grads) * (1.0 / tile)
        wgo[cols, :] = total[:, 0:quarter].astype(BF16)
        wuo[cols, :] = total[:, quarter:].astype(BF16)

    out_g = pltpu.make_async_copy(wgo, ggrad.at[0], l_wg.at[0])
    out_u = pltpu.make_async_copy(wuo, ugrad.at[0], l_wg.at[1])
    out_g.start()
    out_u.start()

    hid_copies = []
    for j in range(2):
        arrived(hb.at[j], r_hid.at[j])
        hv[2 * j, :, :] = (hv[2 * j].astype(F32) + hb[j].astype(F32)).astype(BF16)
        gh = hi if j == 0 else 1 - hi
        for part in range(2):
            group = gh * 2 + (c if part == 0 else 1 - c)
            cp = pltpu.make_async_copy(
                hv.at[2 * j, pl.ds(part * tile, tile)], hid.at[group], l_hid.at[2 * j + part]
            )
            cp.start()
            hid_copies.append(cp)

    @pl.when(even)
    def _():
        for k in range(K):
            zq(1, k).wait_recv()
            if k >= hk:
                merge(zc.at[1], chunk(k), chunk(k - hk), 1)
            fin_of(1, k, zc.at[1, chunk(k)]).start()

    dt_copies = []
    for k in range(K):
        arrived(fin.at[0, chunk(k)], r_fin.at[k])
        arrived(fin.at[1, chunk(k)], r_fin.at[K + k])
        r = chunk(k)
        po[0, r, :] = (po[0, r, :].astype(F32) + fin[0, r, :].astype(F32) + fin[1, r, :].astype(F32)).astype(BF16)
        cp = pltpu.make_async_copy(po.at[0, r], dtok.at[0, r], l_dt.at[k])
        cp.start()
        dt_copies.append(cp)

    for k in range(K):
        ring1(k, tok.at[0, chunk(k)], *to1).wait_send()
        ring3(k, tok.at[0, chunk(k)], *to3).wait_send()
        if k < hk:
            opp1(k).wait_send()
        else:
            opp3(k).wait_send()
        for j in range(2):
            sent(fin.at[j, chunk(k)], s_fin.at[K * j + k])
    cot1.wait_send()
    cot3.wait_send()
    cot_opp.wait_send()
    for s in range(4):
        sib_x(s).wait_send()
        sib_c(s).wait_send()
        sib_ps(s).wait_send()
    for j in range(2):
        hid_of(j).wait_send()
        m_of(j).wait_send()

    @pl.when(even)
    def _():
        cot_z1.wait_send()
        cot_z3.wait_send()
        for k in range(K):
            z1(k).wait_send()
            z3(k).wait_send()
            for j in range(2):
                zq(j, k).wait_send()

    out_g.wait()
    out_u.wait()
    for cp in hid_copies + dt_copies:
        cp.wait()


def per_device(experts, tokens, cotangent, gate_weights, tile_expert, w_gate, w_up):
    _, tile, width = tokens.shape
    quarter = w_gate.shape[2]
    groups = gate_weights.shape[0]
    half = 2 * quarter
    hbm = pl.BlockSpec(memory_space=pl.ANY)
    dma = pltpu.SemaphoreType.DMA
    return pl.pallas_call(
        functools.partial(kernel, experts),
        out_shape=(
            jax.ShapeDtypeStruct(tokens.shape, BF16),
            jax.ShapeDtypeStruct((groups, tile, quarter), BF16),
            jax.ShapeDtypeStruct(w_gate.shape, BF16),
            jax.ShapeDtypeStruct(w_up.shape, BF16),
        ),
        in_specs=[hbm, hbm, hbm, pl.BlockSpec(memory_space=pltpu.SMEM), hbm, hbm],
        out_specs=(hbm, hbm, hbm, hbm),
        scratch_shapes=[
            pltpu.VMEM((5, 2 * tile, width), BF16),
            pltpu.VMEM((6, tile, half), BF16),
            pltpu.VMEM((4, tile, quarter), BF16),
            pltpu.VMEM((2, groups, tile), F32),
            pltpu.VMEM((width, quarter), BF16),
            pltpu.VMEM((width, quarter), BF16),
            pltpu.VMEM((4, 2 * tile, half), BF16),
            pltpu.VMEM((4, 2 * tile, quarter), BF16),
            pltpu.VMEM((2, 2 * tile, quarter), BF16),
            pltpu.VMEM((4, tile, width), BF16),
            pltpu.VMEM((4, tile, width), BF16),
            pltpu.VMEM((4, tile, width), BF16),
            pltpu.VMEM((2, tile // 2, width), BF16),
            pltpu.VMEM((2, tile, width), BF16),
            pltpu.VMEM((2, tile, width), BF16),
            pltpu.VMEM((width, quarter), BF16),
            pltpu.VMEM((width, quarter), BF16),
            dma((2 * K,)), dma((2 * K,)),
            dma((K,)), dma((K,)),
            dma((2 * K,)), dma((2 * K,)),
            dma((4,)), dma((4,)),
            dma((9,)), dma((9,)),
            dma((4,)), dma((4,)),
            dma((2,)), dma((2,)),
            dma((2 * K,)), dma((2 * K,)),
            dma((2 * K,)), dma((2 * K,)),
            dma((2,)), dma((2,)),
            dma((4,)), dma((2,)), dma((4,)), dma((2,)), dma((K,)),
        ],
        compiler_params=pltpu.CompilerParams(
            collective_id=0, has_side_effects=True, vmem_limit_bytes=60 << 20
        ),
    )(tokens, cotangent, gate_weights, tile_expert, w_gate, w_up)


def solution(mesh):
    placed = (
        P("dp", "expert", None),
        P("dp", "expert", None),
        P(),
        P(),
        P("expert", None, "dp"),
        P("expert", None, "dp"),
    )
    return jax.shard_map(
        functools.partial(per_device, mesh.shape["expert"]),
        mesh=mesh,
        in_specs=placed,
        out_specs=(
            P("dp", "expert", None),
            P(None, "expert", "dp"),
            P("expert", None, "dp"),
            P("expert", None, "dp"),
        ),
        check_vma=False,
    )
```

time: 265 us -> 113 us (0.43)
  the two profiles are of different devices: /device:TPU:1 before, /device:TPU:238 now
where the time goes in v1:
time: 113 us
  Pallas kernels  105 us (93%)
  local copies, waits for them, and re-layouts  7.36 us (7%)
    pallas_call x1, Pallas kernels, per_device(): pl.pallas_call(functools.partial(kernel, experts), out_shape=(jax.ShapeDt...  105 us
    unnamed x8, local copies, waits for them, and re-layouts  7.36 us

profile of v1, /device:TPU:238, one launch (start us, length us, event | category | flops | bytes accessed | tf_op | source)
XLA Modules:
  0.0 112.7 jit_solution(10947350318631328388)
XLA Ops:
  0.6 104.7 %shard_map.93 = (bf16[1,128,3584]{2,1,0:T(8,128)(2,1)}, bf16[4,128,256]{2,1,0:T(8,128)(2,1)}, bf16[1,3584,256]{2,1,0:T(8,128)(2,1)}, bf16[1,3584,256]{2,1,0:T(8,128)(2,1)}) custom-call(bf16[1,128,3584]{2,1,0:T(8,128)(2,1)} %tok.1, bf16[1,128,1024]{2,1,0:T(8,128)(2,1)} %cot.1, f32[4,8192]{1,0:T(4,128)} %gw.1, s32[4,64]{1,0:T(4,128)} %te.1, ...), custom_call_target="tpu_custom_call" | custom-call | tf_op jit(solution)/shard_map/pallas_call | solution.py:516
  105.3 0.0 copy-start.1
  105.3 2.3 %copy.14 = bf16[1,128,3584]{2,1,0:T(8,128)(2,1)} copy(bf16[1,128,3584]{2,1,0:T(8,128)(2,1)} %get-tuple-element.8) | data formatting | bytes 1835008
  107.6 1.7 %copy.15 = bf16[4,128,256]{2,1,0:T(8,128)(2,1)} copy(bf16[4,128,256]{2,1,0:T(8,128)(2,1)} %get-tuple-element.9) | data formatting | bytes 524288
  109.3 0.0 copy-done.1
  109.3 0.0 copy-start
  109.3 1.2 %copy.16 = bf16[1,3584,256]{2,1,0:T(8,128)(2,1)} copy(bf16[1,3584,256]{2,1,0:T(8,128)(2,1)S(1)} %copy-done.1) | data formatting | bytes 3670016
  110.5 0.9 copy-done
  111.4 1.2 %copy.17 = bf16[1,3584,256]{2,1,0:T(8,128)(2,1)} copy(bf16[1,3584,256]{2,1,0:T(8,128)(2,1)S(1)} %copy-done) | data formatting | bytes 3670016
Async XLA Ops:
  105.3 4.0 %copy-start.1 = (bf16[1,3584,256]{2,1,0:T(8,128)(2,1)S(1)}, bf16[1,3584,256]{2,1,0:T(8,128)(2,1)}, u32[]{:S(2)}) copy-start(bf16[1,3584,256]{2,1,0:T(8,128)(2,1)} %get-tuple-element.10) | copy-start | bytes 5505028
  109.3 2.2 %copy-start = (bf16[1,3584,256]{2,1,0:T(8,128)(2,1)S(1)}, bf16[1,3584,256]{2,1,0:T(8,128)(2,1)}, u32[]{:S(2)}) copy-start(bf16[1,3584,256]{2,1,0:T(8,128)(2,1)} %get-tuple-element.11) | copy-start | bytes 5505028

commit v2 on v1

v2 whole, which is shorter than its diff:
```python
import functools

import jax
import jax.numpy as jnp
from jax import lax
from jax.experimental import pallas as pl
from jax.experimental.pallas import tpu as pltpu
from jax.sharding import PartitionSpec as P

MESH = pl.DeviceIdType.MESH
F32 = jnp.float32
BF16 = jnp.bfloat16
K = 4
N_COLS = 512


def dot_nn(a, b):
    return lax.dot_general(a, b, (((1,), (0,)), ((), ())), preferred_element_type=F32)


def dot_nt(a, b):
    return lax.dot_general(a, b, (((1,), (1,)), ((), ())), preferred_element_type=F32)


def dot_tn(a, b):
    return lax.dot_general(a, b, (((0,), (0,)), ((), ())), preferred_element_type=F32)


def kernel(
    experts,
    tok, cot, gw, te, wg_hbm, wu_hbm,
    dtok, hid, ggrad, ugrad,
    xr, ch, cs, gwv, wg, wu, gu, hv, hb, po, ps, sp, mv, zc, fin, rl,
    s_ring, r_relay, r_x, s_opp, r_opp, s_z, s_sib, r_sib,
    s_cot, r_cot, s_ps, r_ps, s_m, r_m, s_zc, r_zc, s_fin, r_fin, s_leg, r_leg, r_fin2, s_hid, r_hid,
    l_in, l_gw,
):
    tile = tok.shape[1]
    width = tok.shape[2]
    quarter = wg_hbm.shape[2]
    half = 2 * quarter
    rows = tile // K
    d = lax.axis_index("dp")
    e = lax.axis_index("expert")
    hi, c = d // 2, d % 2
    lo = e % 2
    prev = (e + experts - 1) % experts

    y_e = e + 1 - 2 * lo
    yp = ((d + 2 * lo) % 4, y_e)
    ym = ((d + 2 * (1 - lo)) % 4, y_e)
    opp = ((d + 2) % 4, e)
    sib = (d + 1 - 2 * c, e)
    zn = (d, (e + 2) % experts)
    zp = (d, (e + experts - 2) % experts)
    nxt = (d, (e + 1) % experts)
    nx2 = ((d + 2) % 4, (e + 1) % experts)
    prv = (d, prev)
    pr2 = ((d + 2) % 4, prev)

    def remote(src, dst, send, recv, dev):
        return pltpu.make_async_remote_copy(
            src_ref=src, dst_ref=dst, send_sem=send, recv_sem=recv, device_id=dev, device_id_type=MESH
        )

    def arrived(dst, recv):
        remote(dst, dst, s_m.at[0], recv, sib).wait_recv()

    def sent(src, send):
        remote(src, src, send, r_m.at[0], sib).wait_send()

    def chunk(k, base=0, count=1):
        return pl.ds(base + k * rows, rows * count)

    even = lo == 0
    odd = lo == 1

    own_x = pltpu.make_async_copy(tok.at[0], xr.at[0, pl.ds(0, tile)], l_in.at[0])
    own_c = pltpu.make_async_copy(
        cot.at[0, :, pl.ds(pl.multiple_of(hi * half, half), half)], ch.at[0], l_in.at[1]
    )
    load_g = pltpu.make_async_copy(wg_hbm.at[0], wg, l_in.at[2])
    load_u = pltpu.make_async_copy(wu_hbm.at[0], wu, l_in.at[3])
    gw_own = pltpu.make_async_copy(gw.at[:, pl.ds(pl.multiple_of(e * tile, tile), tile)], gwv.at[0], l_gw.at[0])
    gw_prev = pltpu.make_async_copy(
        gw.at[:, pl.ds(pl.multiple_of(prev * tile, tile), tile)], gwv.at[1], l_gw.at[1]
    )
    own_x.start()
    own_c.start()
    load_g.start()
    load_u.start()
    gw_own.start()
    gw_prev.start()

    barrier = pltpu.get_barrier_semaphore()

    def greet(devices):
        for dev in devices:
            pl.semaphore_signal(barrier, inc=1, device_id=dev, device_id_type=MESH)
        pl.semaphore_wait(barrier, 7)

    mine = pl.ds(pl.multiple_of(c * quarter, quarter), quarter)
    other = pl.ds(pl.multiple_of((1 - c) * quarter, quarter), quarter)

    def cot_half(h, slot, i, dev):
        h = lax.rem(h, 2)
        return remote(
            cot.at[0, :, pl.ds(pl.multiple_of(h * half, half), half)],
            ch.at[slot], s_cot.at[i], r_cot.at[slot], dev,
        )

    def tile_to(k, slot, base, i, recv, dev):
        return remote(tok.at[0, chunk(k)], xr.at[slot, chunk(k, base)], s_ring.at[i], recv, dev)

    hk = K // 2
    first = range(hk)
    second = range(hk, K)
    up_order = list(range(K))
    down_order = up_order[::-1]

    def even_ring1(k):
        return tile_to(k, 1, 0, k, r_x.at[k], yp)

    def even_ring3(k):
        return tile_to(k, 3, 0, K + k, r_x.at[K + k], ym)

    even_cots = [cot_half(hi, 1, 0, yp), cot_half(hi + 1, 3, 1, ym), cot_half(hi + 1, 2, 2, opp)]

    def odd_ring(k):
        if k < hk:
            return tile_to(k, 4, 0, k, r_relay.at[k], yp)
        return tile_to(k, 4, tile, k, r_relay.at[k], ym)

    def odd_up(k):
        if k < hk:
            return tile_to(k, 3, 0, K + k, r_x.at[K + k], nxt)
        return tile_to(k, 1, 0, K + k, r_x.at[k], nx2)

    odd_cots = [cot_half(hi, 3, 0, nxt), cot_half(hi + 1, 1, 1, nx2), cot_half(hi + 1, 2, 2, opp)]

    @pl.when(even)
    def _():
        greet((yp, ym, sib, zn, zp, opp, prv, pr2))
        for k in range(K):
            even_ring1(up_order[k]).start()
            even_ring3(down_order[k]).start()
            if k == 1:
                for copy in even_cots:
                    copy.start()

    @pl.when(odd)
    def _():
        greet((yp, ym, sib, opp, zn, nxt))
        for k in range(hk):
            odd_ring(up_order[k]).start()
            odd_ring(down_order[k]).start()
            odd_up(hk + k).start()
            odd_up(hk - 1 - k).start()
        for copy in odd_cots:
            copy.start()

    def sib_x(s):
        return remote(xr.at[s, pl.ds(0, tile)], xr.at[s, pl.ds(tile, tile)], s_sib.at[s], r_sib.at[s], sib)

    def sib_c(s):
        return remote(ch.at[s, :, other], cs.at[s], s_cot.at[3 + s], r_cot.at[4 + s], sib)

    def to_sibling(s):
        sib_x(s).start()
        sib_c(s).start()

    def from_sibling(s):
        sib_x(s).wait_recv()
        sib_c(s).wait_recv()

    own_x.wait()
    own_c.wait()
    to_sibling(0)

    eye = lax.broadcasted_iota(jnp.int32, (tile, tile), 0) == lax.broadcasted_iota(jnp.int32, (tile, tile), 1)
    gw_own.wait()
    gw_prev.wait()

    def scale_of(group, place, which):
        line = gwv[which, pl.ds(group, 1), :]
        routed = jnp.where(te[group, place] == e, jnp.float32(1.0), jnp.float32(0.0))
        spread = jnp.where(eye, jnp.broadcast_to(line, (tile, tile)), jnp.float32(0.0))
        return jnp.sum(spread, axis=1, keepdims=True) * routed

    def group_half(s):
        return (hi, (hi + 1 - lo) % 2, 1 - hi, (hi + lo) % 2)[s]

    def forward(s):
        gh = group_half(s)
        place, which = (e, 0) if s % 2 == 0 else (prev, 1)
        x = xr[s]
        gate = dot_nn(x, wg[...])
        up = dot_nn(x, wu[...])
        for part in range(2):
            group = gh * 2 + (c if part == 0 else 1 - c)
            w = scale_of(group, place, which)
            r = slice(part * tile, (part + 1) * tile)
            dh = (ch[s, :, mine] if part == 0 else cs[s]).astype(F32)
            g, u = gate[r], up[r]
            sg = jax.nn.sigmoid(g)
            act = g * sg
            hv[s, r, :] = ((w * act) * u).astype(BF16)
            ag = w * dh
            gu[s, r, 0:quarter] = (ag * u * sg * (1.0 + g * (1.0 - sg))).astype(BF16)
            gu[s, r, quarter:half] = (ag * act).astype(BF16)

    def input_grad(dyn):
        gg = gu[dyn, :, 0:quarter]
        ug = gu[dyn, :, quarter:half]

        @pl.loop(0, width // N_COLS)
        def _(n):
            cols = pl.ds(pl.multiple_of(n * N_COLS, N_COLS), N_COLS)
            part = dot_nt(gg, wg[cols, :]) + dot_nt(ug, wu[cols, :])
            po[dyn, :, cols] = part[0:tile].astype(BF16)
            ps[dyn, :, cols] = part[tile:].astype(BF16)

    def sib_ps(s):
        return remote(ps.at[s], sp.at[s], s_ps.at[s], r_ps.at[s], sib)

    def contribution(s):
        sib_ps(s).wait_recv()

        @pl.loop(0, K)
        def _(k):
            r = pl.ds(pl.multiple_of(k * rows, rows), rows)
            po[s, r, :] = (po[s, r, :].astype(F32) + sp[s, r, :].astype(F32)).astype(BF16)

    def relay_z(k):
        if k < hk:
            return remote(xr.at[4, chunk(k)], xr.at[1, chunk(k)], s_z.at[k], r_x.at[k], zn)
        return remote(xr.at[4, chunk(k, tile)], xr.at[3, chunk(k)], s_z.at[k], r_x.at[K + k], zn)

    def relay_opp(k, src_slot, base):
        src = xr.at[src_slot, chunk(k, base)]
        return remote(src, xr.at[2, chunk(k)], s_opp.at[k], r_opp.at[k], yp if k < hk else ym)

    def even_opp(k):
        return relay_opp(k, 4, 0 if k < hk else tile)

    def odd_opp(k):
        return relay_opp(k, 1 if k < hk else 3, 0)

    def got_relay(k):
        arrived(xr.at[4, chunk(k, 0 if k < hk else tile)], r_relay.at[k])

    def got_x(s, k):
        arrived(xr.at[s, chunk(k)], r_x.at[(0 if s == 1 else K) + k])

    def got_cot(s):
        arrived(ch.at[s], r_cot.at[s])

    def got_opp():
        for k in range(K):
            arrived(xr.at[2, chunk(k)], r_opp.at[k])
        got_cot(2)

    def m_of(j):
        r = chunk(j * hk, 0, hk)
        return remote(po.at[2, r], mv.at[j], s_m.at[j], r_m.at[j], ym if j == 0 else yp)

    def fin_of(j, k, src):
        return remote(src, fin.at[j, chunk(k)], s_fin.at[K * j + k], r_fin.at[K * j + k], ym if j == 0 else yp)

    def zq(j, k):
        return remote(po.at[1 + 2 * j, chunk(k)], zc.at[j, chunk(k - j * hk)], s_zc.at[k], r_zc.at[k], zp)

    def leg(j):
        r = chunk((1 - j) * hk, 0, hk)
        return remote(po.at[1 + 2 * j, r], rl.at[j], s_leg.at[j], r_leg.at[j], ym if j == 0 else yp)

    def leg_on(j):
        r = chunk((1 - j) * hk, 0, hk)
        return remote(rl.at[j], fin.at[j, r], s_leg.at[j], r_fin2.at[j], zp)

    def hid_of(j):
        dst = (1 - lo) if j == 0 else lo
        return remote(hv.at[1 + 2 * j], hb.at[dst], s_hid.at[j], r_hid.at[dst], prv)

    def merge(dst, r, m_rows, m_slot):
        dst[r, :] = (dst[r, :].astype(F32) + mv[m_slot, m_rows, :].astype(F32)).astype(BF16)

    def weight_grads():
        @pl.loop(0, width // N_COLS)
        def _(n):
            cols = pl.ds(pl.multiple_of(n * N_COLS, N_COLS), N_COLS)
            x = xr[0:4, :, cols].reshape(8 * tile, N_COLS)
            grads = gu[...].reshape(8 * tile, half)
            total = dot_tn(x, grads) * (1.0 / tile)
            ggrad[0, cols, :] = total[:, 0:quarter].astype(BF16)
            ugrad[0, cols, :] = total[:, quarter:].astype(BF16)

    def hidden_out():
        for j in range(2):
            arrived(hb.at[j], r_hid.at[j])
            gh = hi if j == 0 else 1 - hi
            for part in range(2):
                group = gh * 2 + (c if part == 0 else 1 - c)
                r = slice(part * tile, (part + 1) * tile)
                hid[group, :, :] = (hv[2 * j, r, :].astype(F32) + hb[j, r, :].astype(F32)).astype(BF16)

    def total(k):
        r = chunk(k)
        dtok[0, r, :] = (po[0, r, :].astype(F32) + fin[0, r, :].astype(F32) + fin[1, r, :].astype(F32)).astype(BF16)

    load_g.wait()
    load_u.wait()

    @pl.when(even)
    def _():
        from_sibling(0)
        forward(0)
        for k in (0, K - 1):
            got_relay(k)
            relay_z(k).start()
            even_opp(k).start()
        input_grad(0)
        sib_ps(0).start()
        for k in (1, K - 2):
            got_relay(k)
            relay_z(k).start()
            even_opp(k).start()
        contribution(0)
        for s in (1, 3):
            got_cot(s)
            for k in range(K):
                got_x(s, k)
            to_sibling(s)
        from_sibling(1)
        forward(1)
        input_grad(1)
        sib_ps(1).start()
        hid_of(0).start()
        from_sibling(3)
        forward(3)
        hid_of(1).start()
        contribution(1)
        leg(0).start()
        for k in first:
            zq(0, k).start()
        input_grad(3)
        sib_ps(3).start()
        got_opp()
        to_sibling(2)
        contribution(3)
        leg(1).start()
        for k in second:
            zq(1, k).start()
        from_sibling(2)
        forward(2)
        input_grad(2)
        sib_ps(2).start()
        contribution(2)
        m_of(0).start()
        m_of(1).start()
        for j in range(2):
            m_of(j).wait_recv()
            for i in range(hk):
                k = j * hk + i
                zq(j, k).wait_recv()
                merge(zc.at[j], chunk(i), chunk(i), j)
                fin_of(j, k, zc.at[j, chunk(i)]).start()
        weight_grads()
        hidden_out()
        for k in range(K):
            for j in range(2):
                arrived(fin.at[j, chunk(k)], r_fin.at[K * j + k])
            total(k)
        for k in range(K):
            even_ring1(k).wait_send()
            even_ring3(k).wait_send()
            relay_z(k).wait_send()
            even_opp(k).wait_send()
            zq(k // hk, k).wait_send()
            fin_of(k // hk, k, zc.at[k // hk, chunk(k % hk)]).wait_send()
        for copy in even_cots:
            copy.wait_send()
        for j in range(2):
            leg(j).wait_send()

    @pl.when(odd)
    def _():
        from_sibling(0)
        forward(0)
        for k in (0, K - 1):
            got_x(1 if k < hk else 3, k)
            odd_opp(k).start()
        input_grad(0)
        sib_ps(0).start()
        for k in (1, K - 2):
            got_x(1 if k < hk else 3, k)
            odd_opp(k).start()
        contribution(0)
        for s in (1, 3):
            got_cot(s)
            for k in second if s == 1 else first:
                got_x(s, k)
            to_sibling(s)
        from_sibling(1)
        forward(1)
        input_grad(1)
        sib_ps(1).start()
        hid_of(0).start()
        from_sibling(3)
        forward(3)
        hid_of(1).start()
        contribution(1)
        for k in second:
            fin_of(0, k, po.at[1, chunk(k)]).start()
        input_grad(3)
        sib_ps(3).start()
        got_opp()
        to_sibling(2)
        contribution(3)
        for k in first:
            fin_of(1, k, po.at[3, chunk(k)]).start()
        from_sibling(2)
        forward(2)
        input_grad(2)
        sib_ps(2).start()
        contribution(2)
        m_of(0).start()
        m_of(1).start()
        for j in range(2):
            leg(j).wait_recv()
            leg_on(j).start()
        for j in range(2):
            m_of(j).wait_recv()
            for i in range(hk):
                k = j * hk + i
                src = po.at[1 + 2 * j]
                merge(src, chunk(k), chunk(i), j)
                fin_of(j, k, src.at[chunk(k)]).start()
        weight_grads()
        hidden_out()
        for j in range(2):
            r = chunk((1 - j) * hk, 0, hk)
            arrived(fin.at[j, r], r_fin2.at[j])
        for k in range(K):
            arrived(fin.at[k // hk, chunk(k)], r_fin.at[K * (k // hk) + k])
            total(k)
        for k in range(K):
            odd_ring(k).wait_send()
            odd_up(k).wait_send()
            odd_opp(k).wait_send()
            for j in range(2):
                fin_of(j, k, po.at[1 + 2 * j, chunk(k)]).wait_send()
        for copy in odd_cots:
            copy.wait_send()
        for j in range(2):
            leg_on(j).wait_send()

    for s in range(4):
        sib_x(s).wait_send()
        sib_c(s).wait_send()
        sib_ps(s).wait_send()
    for j in range(2):
        hid_of(j).wait_send()
        m_of(j).wait_send()


def store(*refs):
    count = len(refs) // 2
    sem = refs[-1]
    copies = [pltpu.make_async_copy(refs[i], refs[count + i], sem.at[i]) for i in range(count)]
    for copy in copies:
        copy.start()
    for copy in copies:
        copy.wait()


def per_device(experts, tokens, cotangent, gate_weights, tile_expert, w_gate, w_up):
    _, tile, width = tokens.shape
    quarter = w_gate.shape[2]
    groups = gate_weights.shape[0]
    half = 2 * quarter
    hbm = pl.BlockSpec(memory_space=pltpu.HBM)
    dma = pltpu.SemaphoreType.DMA
    vmem = pl.BlockSpec(memory_space=pltpu.VMEM)
    shapes = (tokens.shape, (groups, tile, quarter), w_gate.shape, w_up.shape)
    parts = pl.pallas_call(
        functools.partial(kernel, experts),
        out_shape=tuple(pltpu.VMEM(shape, BF16) for shape in shapes),
        in_specs=[hbm, hbm, hbm, pl.BlockSpec(memory_space=pltpu.SMEM), hbm, hbm],
        out_specs=(vmem, vmem, vmem, vmem),
        scratch_shapes=[
            pltpu.VMEM((5, 2 * tile, width), BF16),
            pltpu.VMEM((4, tile, half), BF16),
            pltpu.VMEM((4, tile, quarter), BF16),
            pltpu.VMEM((2, groups, tile), F32),
            pltpu.VMEM((width, quarter), BF16),
            pltpu.VMEM((width, quarter), BF16),
            pltpu.VMEM((4, 2 * tile, half), BF16),
            pltpu.VMEM((4, 2 * tile, quarter), BF16),
            pltpu.VMEM((2, 2 * tile, quarter), BF16),
            pltpu.VMEM((4, tile, width), BF16),
            pltpu.VMEM((4, tile, width), BF16),
            pltpu.VMEM((4, tile, width), BF16),
            pltpu.VMEM((2, tile // 2, width), BF16),
            pltpu.VMEM((2, tile // 2, width), BF16),
            pltpu.VMEM((2, tile, width), BF16),
            pltpu.VMEM((2, tile // 2, width), BF16),
            dma((2 * K,)), dma((K,)), dma((2 * K,)),
            dma((K,)), dma((K,)),
            dma((K,)),
            dma((4,)), dma((4,)),
            dma((7,)), dma((8,)),
            dma((4,)), dma((4,)),
            dma((2,)), dma((2,)),
            dma((K,)), dma((K,)),
            dma((2 * K,)), dma((2 * K,)),
            dma((2,)), dma((2,)), dma((2,)),
            dma((2,)), dma((2,)),
            dma((4,)), dma((2,)),
        ],
        compiler_params=pltpu.CompilerParams(
            collective_id=0, has_side_effects=True, vmem_limit_bytes=62_192_000
        ),
    )(tokens, cotangent, gate_weights, tile_expert, w_gate, w_up)
    return pl.pallas_call(
        store,
        out_shape=tuple(jax.ShapeDtypeStruct(shape, BF16) for shape in shapes),
        in_specs=[pl.BlockSpec(memory_space=pl.ANY)] * 4,
        out_specs=(hbm, hbm, hbm, hbm),
        scratch_shapes=[dma((4,))],
        compiler_params=pltpu.CompilerParams(vmem_limit_bytes=1 << 20),
    )(*parts)


def solution(mesh):
    placed = (
        P("dp", "expert", None),
        P("dp", "expert", None),
        P(),
        P(),
        P("expert", None, "dp"),
        P("expert", None, "dp"),
    )
    return jax.shard_map(
        functools.partial(per_device, mesh.shape["expert"]),
        mesh=mesh,
        in_specs=placed,
        out_specs=(
            P("dp", "expert", None),
            P(None, "expert", "dp"),
            P("expert", None, "dp"),
            P("expert", None, "dp"),
        ),
        check_vma=False,
    )
```

time: 113 us -> 92.8 us (0.82)
  the two profiles are of different devices: /device:TPU:238 before, /device:TPU:1 now
where the time goes in v2:
time: 92.8 us; the launch traced here: 92.7 us
  Pallas kernels  92.1 us (99%)
    pallas_call x1, Pallas kernels, per_device(): pl.pallas_call(functools.partial(kernel, experts), out_shape=tuple((pltpu...  89.8 us
    pallas_call x1, Pallas kernels, per_device(): pl.pallas_call(store, out_shape=tuple((jax.ShapeDtypeStruct(shape, BF16)...  2.26 us

profile of v2, /device:TPU:1, one launch (start us, length us, event | category | flops | bytes accessed | tf_op | source)
XLA Modules:
  0.0 92.7 jit_solution(12901500366015219252)
XLA Ops:
  0.6 89.8 %shard_map.93 = (bf16[1,128,3584]{2,1,0:T(8,128)(2,1)S(1)}, bf16[4,128,256]{2,1,0:T(8,128)(2,1)S(1)}, bf16[1,3584,256]{2,1,0:T(8,128)(2,1)S(1)}, bf16[1,3584,256]{2,1,0:T(8,128)(2,1)S(1)}) custom-call(bf16[1,128,3584]{2,1,0:T(8,128)(2,1)} %tok.1, bf16[1,128,1024]{2,1,0:T(8,128)(2,1)} %cot.1, f32[4,8192]{1,0:T(4,128)} %gw.1, s32[4,64]{1,0:T(4,128)} %te.1, ...), custom_call_target="tpu_custom_call" | custom-call | tf_op jit(solution)/shard_map/pallas_call | solution.py:486
  90.4 2.3 %shard_map.94 = (bf16[1,128,3584]{2,1,0:T(8,128)(2,1)}, bf16[4,128,256]{2,1,0:T(8,128)(2,1)}, bf16[1,3584,256]{2,1,0:T(8,128)(2,1)}, bf16[1,3584,256]{2,1,0:T(8,128)(2,1)}) custom-call(bf16[1,128,3584]{2,1,0:T(8,128)(2,1)S(1)} %get-tuple-element.8.refs_0_, bf16[4,128,256]{2,1,0:T(8,128)(2,1)S(1)} %get-tuple-element.9.refs_1_, ...), custom_call_target="tpu_custom_call" | custom-call | tf_op jit(solution)/shard_map/pallas_call | solution.py:525

commit v3 on v2

v3 whole, which is shorter than its diff:
```python
import functools

import jax
import jax.numpy as jnp
from jax import lax
from jax.experimental import pallas as pl
from jax.experimental.pallas import tpu as pltpu
from jax.sharding import PartitionSpec as P

MESH = pl.DeviceIdType.MESH
F32 = jnp.float32
BF16 = jnp.bfloat16
K = 4
N_COLS = 512


def dot_nn(a, b):
    return lax.dot_general(a, b, (((1,), (0,)), ((), ())), preferred_element_type=F32)


def dot_nt(a, b):
    return lax.dot_general(a, b, (((1,), (1,)), ((), ())), preferred_element_type=F32)


def dot_tn(a, b):
    return lax.dot_general(a, b, (((0,), (0,)), ((), ())), preferred_element_type=F32)


def kernel(
    experts,
    tok, cot, gw, te, wg_hbm, wu_hbm,
    dtok, hid, ggrad, ugrad,
    xr, xrelay, ch, cs, gwv, wg, wu, gu, hv, hb, po, ps, sp, mv, zc, fin, rl,
    s_ring, r_relay, r_x, s_opp, r_opp, s_z, s_sib, r_sib, s_cot, r_cot, s_sc, r_sc,
    s_ps, r_ps, s_m, r_m, s_zc, r_zc, s_fin, r_fin, s_leg, r_leg, s_hid, r_hid,
    l_in, l_gw,
):
    tile = tok.shape[1]
    width = tok.shape[2]
    quarter = wg_hbm.shape[2]
    half = 2 * quarter
    rows = tile // K
    d = lax.axis_index("dp")
    e = lax.axis_index("expert")
    hi, c = d // 2, d % 2
    lo = e % 2
    prev = (e + experts - 1) % experts

    y_e = e + 1 - 2 * lo
    yp = ((d + 2 * lo) % 4, y_e)
    ym = ((d + 2 * (1 - lo)) % 4, y_e)
    opp = ((d + 2) % 4, e)
    sib = (d + 1 - 2 * c, e)
    zn = (d, (e + 2) % experts)
    zp = (d, (e + experts - 2) % experts)
    nxt = (d, (e + 1) % experts)
    nx2 = ((d + 2) % 4, (e + 1) % experts)
    prv = (d, prev)
    pr2 = ((d + 2) % 4, prev)

    def remote(src, dst, send, recv, dev):
        return pltpu.make_async_remote_copy(
            src_ref=src, dst_ref=dst, send_sem=send, recv_sem=recv, device_id=dev, device_id_type=MESH
        )

    def arrived(dst, recv):
        remote(dst, dst, s_m.at[0], recv, sib).wait_recv()

    def sent(src, send):
        remote(src, src, send, r_m.at[0], sib).wait_send()

    def chunk(k, base=0, count=1):
        return pl.ds(base + k * rows, rows * count)

    even = lo == 0
    odd = lo == 1

    own_x = pltpu.make_async_copy(tok.at[0], xr.at[0, pl.ds(0, tile)], l_in.at[0])
    own_c = pltpu.make_async_copy(
        cot.at[0, :, pl.ds(pl.multiple_of(hi * half, half), half)], ch.at[0], l_in.at[1]
    )
    load_g = pltpu.make_async_copy(wg_hbm.at[0], wg, l_in.at[2])
    load_u = pltpu.make_async_copy(wu_hbm.at[0], wu, l_in.at[3])
    gw_own = pltpu.make_async_copy(gw.at[:, pl.ds(pl.multiple_of(e * tile, tile), tile)], gwv.at[0], l_gw.at[0])
    gw_prev = pltpu.make_async_copy(
        gw.at[:, pl.ds(pl.multiple_of(prev * tile, tile), tile)], gwv.at[1], l_gw.at[1]
    )
    own_x.start()
    own_c.start()
    load_g.start()
    load_u.start()
    gw_own.start()
    gw_prev.start()

    barrier = pltpu.get_barrier_semaphore()

    def greet(devices):
        for dev in devices:
            pl.semaphore_signal(barrier, inc=1, device_id=dev, device_id_type=MESH)
        pl.semaphore_wait(barrier, 7)

    mine = pl.ds(pl.multiple_of(c * quarter, quarter), quarter)
    other = pl.ds(pl.multiple_of((1 - c) * quarter, quarter), quarter)

    hk = K // 2
    pairs = [(i, K - 1 - i) for i in range(hk)]
    order = [k for pair in pairs for k in pair]
    low, high = pl.ds(0, tile // 2), pl.ds(tile // 2, tile // 2)

    def cot_to(h, r, slot, i, recv, dev):
        h = lax.rem(h, 2)
        return remote(
            cot.at[0, r, pl.ds(pl.multiple_of(h * half, half), half)],
            ch.at[slot, r], s_cot.at[i], r_cot.at[recv], dev,
        )

    all_rows = pl.ds(0, tile)
    cot_opp = cot_to(hi + 1, all_rows, 2, 4, 4, opp)

    def x_to(k, slot, i, dev):
        return remote(
            tok.at[0, chunk(k)], xr.at[slot, chunk(k)], s_ring.at[i], r_x.at[(0 if slot == 1 else K) + k], dev
        )

    def even_first(k):
        return x_to(k, 1, k, yp if k < hk else ym)

    def even_last(k):
        return x_to(k, 3, K + k, ym if k < hk else yp)

    even_cots = [
        cot_to(hi, low, 1, 0, 0, yp), cot_to(hi + 1, high, 1, 1, 1, ym),
        cot_to(hi + 1, low, 3, 2, 2, ym), cot_to(hi, high, 3, 3, 3, yp),
    ]

    def odd_ring(k):
        return remote(
            tok.at[0, chunk(k)], xrelay.at[chunk(k)], s_ring.at[k], r_relay.at[k], yp if k < hk else ym
        )

    def odd_up(k):
        return x_to(k, 3, K + k, nxt if k < hk else nx2)

    odd_cots = [
        cot_to(hi + 1, low, 1, 0, 0, nx2), cot_to(hi, high, 1, 1, 1, nxt),
        cot_to(hi, low, 3, 2, 2, nxt), cot_to(hi + 1, high, 3, 3, 3, nx2),
    ]

    @pl.when(even)
    def _():
        greet((yp, ym, sib, zn, zp, opp, prv, pr2))
        for k in order:
            even_first(k).start()

    @pl.when(odd)
    def _():
        greet((yp, ym, sib, opp, zn, nxt))
        for k in order:
            odd_ring(k).start()

    def sib_x(s, k):
        return remote(
            xr.at[s, chunk(k)], xr.at[s, chunk(k, tile)], s_sib.at[K * s + k], r_sib.at[K * s + k], sib
        )

    def sib_c(s):
        return remote(ch.at[s, :, other], cs.at[s], s_sc.at[s], r_sc.at[s], sib)

    def from_sibling(s):
        for k in range(K):
            sib_x(s, k).wait_recv()
        sib_c(s).wait_recv()

    own_x.wait()
    own_c.wait()
    for k in range(K):
        sib_x(0, k).start()
    sib_c(0).start()

    eye = lax.broadcasted_iota(jnp.int32, (tile, tile), 0) == lax.broadcasted_iota(jnp.int32, (tile, tile), 1)
    first_lanes = lax.broadcasted_iota(jnp.int32, (1, tile), 1) < tile // 2
    gw_own.wait()
    gw_prev.wait()

    gh_one = (hi + 1 - lo) % 2
    gh_three = (hi + lo) % 2

    def weights_of(gh, core, place, which):
        group = gh * 2 + core
        routed = jnp.where(te[group, place] == e, jnp.float32(1.0), jnp.float32(0.0))
        return gwv[which, pl.ds(group, 1), :] * routed

    def scale_of(s, core):
        if s % 2 == 0:
            line = weights_of(hi if s == 0 else 1 - hi, core, e, 0)
        else:
            one = weights_of(gh_one, core, prev, 1)
            three = weights_of(gh_three, core, prev, 1)
            line = jnp.where(first_lanes, one, three) if s == 1 else jnp.where(first_lanes, three, one)
        spread = jnp.where(eye, jnp.broadcast_to(line, (tile, tile)), jnp.float32(0.0))
        return jnp.sum(spread, axis=1, keepdims=True)

    def forward(s):
        x = xr[s]
        gate = dot_nn(x, wg[...])
        up = dot_nn(x, wu[...])
        for part in range(2):
            w = scale_of(s, c if part == 0 else 1 - c)
            r = slice(part * tile, (part + 1) * tile)
            dh = (ch[s, :, mine] if part == 0 else cs[s]).astype(F32)
            g, u = gate[r], up[r]
            sg = jax.nn.sigmoid(g)
            act = g * sg
            hv[s, r, :] = ((w * act) * u).astype(BF16)
            ag = w * dh
            gu[s, r, 0:quarter] = (ag * u * sg * (1.0 + g * (1.0 - sg))).astype(BF16)
            gu[s, r, quarter:half] = (ag * act).astype(BF16)

    def sib_ps(s):
        return remote(ps.at[s], sp.at[s], s_ps.at[s], r_ps.at[s], sib)

    def input_grad(s):
        gg = gu[s, :, 0:quarter]
        ug = gu[s, :, quarter:half]

        @pl.loop(0, width // N_COLS)
        def _(n):
            cols = pl.ds(pl.multiple_of(n * N_COLS, N_COLS), N_COLS)
            part = dot_nt(gg, wg[cols, :]) + dot_nt(ug, wu[cols, :])
            po[s, :, cols] = part[0:tile].astype(BF16)
            ps[s, :, cols] = part[tile:].astype(BF16)

        sib_ps(s).start()

    def contribution(s, send=None):
        sib_ps(s).wait_recv()
        for k in order:
            r = chunk(k)
            po[s, r, :] = (po[s, r, :].astype(F32) + sp[s, r, :].astype(F32)).astype(BF16)
            if send is not None:
                send(k).start()

    def relay_z(k):
        return remote(xrelay.at[chunk(k)], xr.at[1, chunk(k)], s_z.at[k], r_x.at[k], zn)

    def relay_opp(k, src):
        return remote(src, xr.at[2, chunk(k)], s_opp.at[k], r_opp.at[k], yp if k < hk else ym)

    def even_opp(k):
        return relay_opp(k, xrelay.at[chunk(k)])

    def odd_opp(k):
        return relay_opp(k, xr.at[1, chunk(k)])

    def got_relay(k):
        arrived(xrelay.at[chunk(k)], r_relay.at[k])

    def got_cot(s):
        if s == 2:
            arrived(ch.at[2], r_cot.at[4])
        else:
            arrived(ch.at[s, low], r_cot.at[s - 1])
            arrived(ch.at[s, high], r_cot.at[s])
        sib_c(s).start()

    def got(s, k):
        arrived(xr.at[s, chunk(k)], r_opp.at[k] if s == 2 else r_x.at[(0 if s == 1 else K) + k])
        sib_x(s, k).start()

    def got_all(s):
        got_cot(s)
        for k in order:
            got(s, k)

    def m_of(k):
        return remote(po.at[2, chunk(k)], mv.at[chunk(k)], s_m.at[k], r_m.at[k], ym if k < hk else yp)

    def fin_a(k, src):
        j = 0 if k < hk else 1
        return remote(
            src.at[chunk(k)], fin.at[j, chunk(k)], s_fin.at[k], r_fin.at[K * j + k], ym if k < hk else yp
        )

    def fin_b(k):
        j = 1 if k < hk else 0
        return remote(
            po.at[3, chunk(k)], fin.at[j, chunk(k)], s_fin.at[K + k], r_fin.at[K * j + k], yp if k < hk else ym
        )

    def zq(k):
        return remote(po.at[1, chunk(k)], zc.at[chunk(k)], s_zc.at[k], r_zc.at[k], zp)

    def leg(k):
        return remote(po.at[3, chunk(k)], rl.at[chunk(k)], s_leg.at[k], r_leg.at[k], yp if k < hk else ym)

    def leg_on(k):
        j = 1 if k < hk else 0
        return remote(rl.at[chunk(k)], fin.at[j, chunk(k)], s_leg.at[k], r_fin.at[K * j + k], zp)

    def hid_of(j):
        return remote(hv.at[1 + 2 * j], hb.at[j], s_hid.at[j], r_hid.at[j], prv)

    def merge(dst, k):
        r = chunk(k)
        dst[r, :] = (dst[r, :].astype(F32) + mv[r, :].astype(F32)).astype(BF16)

    def weight_grads():
        @pl.loop(0, width // N_COLS)
        def _(n):
            cols = pl.ds(pl.multiple_of(n * N_COLS, N_COLS), N_COLS)
            x = xr[:, :, cols].reshape(8 * tile, N_COLS)
            grads = gu[...].reshape(8 * tile, half)
            total = dot_tn(x, grads) * (1.0 / tile)
            ggrad[0, cols, :] = total[:, 0:quarter].astype(BF16)
            ugrad[0, cols, :] = total[:, quarter:].astype(BF16)

    def hidden_out(first):
        for j in range(2):
            hid_of(j).wait_recv()
        for slot in (0, 2):
            gh = hi if slot == 0 else 1 - hi
            lead = first if slot == 0 else 1 - first
            for part in range(2):
                group = gh * 2 + (c if part == 0 else 1 - c)
                for i in range(2):
                    r = slice(part * tile + i * (tile // 2), part * tile + (i + 1) * (tile // 2))
                    back = hb[lead if i == 0 else 1 - lead, r, :]
                    hid[group, i * (tile // 2) : (i + 1) * (tile // 2), :] = (
                        hv[slot, r, :].astype(F32) + back.astype(F32)
                    ).astype(BF16)

    def totals():
        for k in order:
            for j in range(2):
                arrived(fin.at[j, chunk(k)], r_fin.at[K * j + k])
            r = chunk(k)
            dtok[0, r, :] = (po[0, r, :].astype(F32) + fin[0, r, :].astype(F32) + fin[1, r, :].astype(F32)).astype(
                BF16
            )

    load_g.wait()
    load_u.wait()

    @pl.when(even)
    def _():
        for k in [k for i in range(hk) for k in (hk + i, hk - 1 - i)]:
            even_last(k).start()
        for copy in even_cots[2:]:
            copy.start()
        for copy in even_cots[:2]:
            copy.start()
        cot_opp.start()
        from_sibling(0)
        forward(0)
        for k in order[:hk]:
            got_relay(k)
            relay_z(k).start()
            even_opp(k).start()
        input_grad(0)
        for k in order[hk:]:
            got_relay(k)
            relay_z(k).start()
            even_opp(k).start()
        contribution(0)
        got_all(3)
        from_sibling(3)
        forward(3)
        hid_of(1).start()
        input_grad(3)
        got_all(1)
        contribution(3, leg)
        from_sibling(1)
        forward(1)
        hid_of(0).start()
        input_grad(1)
        got_all(2)
        contribution(1, zq)
        from_sibling(2)
        forward(2)
        input_grad(2)
        contribution(2, m_of)
        for k in order:
            m_of(k).wait_recv()
            zq(k).wait_recv()
            merge(zc, k)
            fin_a(k, zc).start()
        weight_grads()
        hidden_out(0)
        totals()
        for k in range(K):
            even_first(k).wait_send()
            even_last(k).wait_send()
            relay_z(k).wait_send()
            even_opp(k).wait_send()
            zq(k).wait_send()
            leg(k).wait_send()
            fin_a(k, zc).wait_send()
        for copy in even_cots:
            copy.wait_send()

    @pl.when(odd)
    def _():
        for k in order:
            odd_up(k).start()
        for copy in odd_cots[2:]:
            copy.start()
        for copy in odd_cots[:2]:
            copy.start()
        cot_opp.start()
        from_sibling(0)
        forward(0)
        for k in order[:hk]:
            got(1, k)
            odd_opp(k).start()
        input_grad(0)
        for k in order[hk:]:
            got(1, k)
            odd_opp(k).start()
        got_cot(1)
        contribution(0)
        from_sibling(1)
        forward(1)
        hid_of(0).start()
        input_grad(1)
        got_all(3)
        contribution(1)
        from_sibling(3)
        forward(3)
        hid_of(1).start()
        input_grad(3)
        got_all(2)
        contribution(3, fin_b)
        from_sibling(2)
        forward(2)
        input_grad(2)
        for k in order:
            leg(k).wait_recv()
            leg_on(k).start()
        contribution(2, m_of)
        for k in order:
            m_of(k).wait_recv()
            merge(po.at[1], k)
            fin_a(k, po.at[1]).start()
        weight_grads()
        hidden_out(1)
        totals()
        for k in range(K):
            odd_ring(k).wait_send()
            odd_up(k).wait_send()
            odd_opp(k).wait_send()
            fin_a(k, po.at[1]).wait_send()
            fin_b(k).wait_send()
            leg_on(k).wait_send()
        for copy in odd_cots:
            copy.wait_send()

    cot_opp.wait_send()
    for s in range(4):
        for k in range(K):
            sib_x(s, k).wait_send()
        sib_c(s).wait_send()
        sib_ps(s).wait_send()
    for k in range(K):
        m_of(k).wait_send()
    for j in range(2):
        hid_of(j).wait_send()


def store(*refs):
    count = len(refs) // 2
    sem = refs[-1]
    copies = [pltpu.make_async_copy(refs[i], refs[count + i], sem.at[i]) for i in range(count)]
    for copy in copies:
        copy.start()
    for copy in copies:
        copy.wait()


def per_device(experts, tokens, cotangent, gate_weights, tile_expert, w_gate, w_up):
    _, tile, width = tokens.shape
    quarter = w_gate.shape[2]
    groups = gate_weights.shape[0]
    half = 2 * quarter
    hbm = pl.BlockSpec(memory_space=pltpu.HBM)
    dma = pltpu.SemaphoreType.DMA
    vmem = pl.BlockSpec(memory_space=pltpu.VMEM)
    shapes = (tokens.shape, (groups, tile, quarter), w_gate.shape, w_up.shape)
    parts = pl.pallas_call(
        functools.partial(kernel, experts),
        out_shape=tuple(pltpu.VMEM(shape, BF16) for shape in shapes),
        in_specs=[hbm, hbm, hbm, pl.BlockSpec(memory_space=pltpu.SMEM), hbm, hbm],
        out_specs=(vmem, vmem, vmem, vmem),
        scratch_shapes=[
            pltpu.VMEM((4, 2 * tile, width), BF16),
            pltpu.VMEM((tile, width), BF16),
            pltpu.VMEM((4, tile, half), BF16),
            pltpu.VMEM((4, tile, quarter), BF16),
            pltpu.VMEM((2, groups, tile), F32),
            pltpu.VMEM((width, quarter), BF16),
            pltpu.VMEM((width, quarter), BF16),
            pltpu.VMEM((4, 2 * tile, half), BF16),
            pltpu.VMEM((4, 2 * tile, quarter), BF16),
            pltpu.VMEM((2, 2 * tile, quarter), BF16),
            pltpu.VMEM((4, tile, width), BF16),
            pltpu.VMEM((4, tile, width), BF16),
            pltpu.VMEM((4, tile, width), BF16),
            pltpu.VMEM((tile, width), BF16),
            pltpu.VMEM((tile, width), BF16),
            pltpu.VMEM((2, tile, width), BF16),
            pltpu.VMEM((tile, width), BF16),
            dma((2 * K,)), dma((K,)), dma((2 * K,)),
            dma((K,)), dma((K,)),
            dma((K,)),
            dma((4 * K,)), dma((4 * K,)),
            dma((5,)), dma((5,)), dma((4,)), dma((4,)),
            dma((4,)), dma((4,)),
            dma((K,)), dma((K,)),
            dma((K,)), dma((K,)),
            dma((2 * K,)), dma((2 * K,)),
            dma((K,)), dma((K,)),
            dma((2,)), dma((2,)),
            dma((4,)), dma((2,)),
        ],
        compiler_params=pltpu.CompilerParams(
            collective_id=0, has_side_effects=True, vmem_limit_bytes=62_192_000
        ),
    )(tokens, cotangent, gate_weights, tile_expert, w_gate, w_up)
    return pl.pallas_call(
        store,
        out_shape=tuple(jax.ShapeDtypeStruct(shape, BF16) for shape in shapes),
        in_specs=[pl.BlockSpec(memory_space=pl.ANY)] * 4,
        out_specs=(hbm, hbm, hbm, hbm),
        scratch_shapes=[dma((4,))],
        compiler_params=pltpu.CompilerParams(vmem_limit_bytes=1 << 20),
    )(*parts)


def solution(mesh):
    placed = (
        P("dp", "expert", None),
        P("dp", "expert", None),
        P(),
        P(),
        P("expert", None, "dp"),
        P("expert", None, "dp"),
    )
    return jax.shard_map(
        functools.partial(per_device, mesh.shape["expert"]),
        mesh=mesh,
        in_specs=placed,
        out_specs=(
            P("dp", "expert", None),
            P(None, "expert", "dp"),
            P("expert", None, "dp"),
            P("expert", None, "dp"),
        ),
        check_vma=False,
    )
```

time: 92.8 us -> 89.3 us (0.962)
  Pallas kernels: 92.1 us -> 88.4 us
    pallas_call x1, Pallas kernels: 89.8 us -> 86.1 us  [per_device(): pl.pallas_call(functools.partial(kernel, experts), out_shape=tuple((pltpu...]
where the time goes in v3:
time: 89.3 us; the launch traced here: 89.2 us
  Pallas kernels  88.4 us (99%)
    pallas_call x1, Pallas kernels, per_device(): pl.pallas_call(functools.partial(kernel, experts), out_shape=tuple((pltpu...  86.1 us
    pallas_call x1, Pallas kernels, per_device(): pl.pallas_call(store, out_shape=tuple((jax.ShapeDtypeStruct(shape, BF16)...  2.26 us

profile of v3, /device:TPU:1, one launch (start us, length us, event | category | flops | bytes accessed | tf_op | source)
XLA Modules:
  0.0 89.2 jit_solution(11834551371852103269)
XLA Ops:
  0.6 86.1 %shard_map.93 = (bf16[1,128,3584]{2,1,0:T(8,128)(2,1)S(1)}, bf16[4,128,256]{2,1,0:T(8,128)(2,1)S(1)}, bf16[1,3584,256]{2,1,0:T(8,128)(2,1)S(1)}, bf16[1,3584,256]{2,1,0:T(8,128)(2,1)S(1)}) custom-call(bf16[1,128,3584]{2,1,0:T(8,128)(2,1)} %tok.1, bf16[1,128,1024]{2,1,0:T(8,128)(2,1)} %cot.1, f32[4,8192]{1,0:T(4,128)} %gw.1, s32[4,64]{1,0:T(4,128)} %te.1, ...), custom_call_target="tpu_custom_call" | custom-call | tf_op jit(solution)/shard_map/pallas_call | solution.py:488
  86.8 2.3 %shard_map.94 = (bf16[1,128,3584]{2,1,0:T(8,128)(2,1)}, bf16[4,128,256]{2,1,0:T(8,128)(2,1)}, bf16[1,3584,256]{2,1,0:T(8,128)(2,1)}, bf16[1,3584,256]{2,1,0:T(8,128)(2,1)}) custom-call(bf16[1,128,3584]{2,1,0:T(8,128)(2,1)S(1)} %get-tuple-element.8.refs_0_, bf16[4,128,256]{2,1,0:T(8,128)(2,1)S(1)} %get-tuple-element.9.refs_1_, ...), custom_call_target="tpu_custom_call" | custom-call | tf_op jit(solution)/shard_map/pallas_call | solution.py:528

commit v4 on v3

--- a/solution.py
+++ b/solution.py
@@ -156,6 +156,7 @@
     def _():
         greet((yp, ym, sib, opp, zn, nxt))
         for k in order:
+            odd_up(k).start()
             odd_ring(k).start()
 
     def sib_x(s, k):
@@ -400,8 +401,6 @@
 
     @pl.when(odd)
     def _():
-        for k in order:
-            odd_up(k).start()
         for copy in odd_cots[2:]:
             copy.start()
         for copy in odd_cots[:2]:

time: 89.3 us -> 88.8 us (level)
  no operation moved by 1% of the time
where the time goes in v4:
time: 88.8 us; the launch traced here: 88.7 us
  Pallas kernels  87.9 us (99%)
    pallas_call x1, Pallas kernels, per_device(): pl.pallas_call(functools.partial(kernel, experts), out_shape=tuple((pltpu...  85.7 us
    pallas_call x1, Pallas kernels, per_device(): pl.pallas_call(store, out_shape=tuple((jax.ShapeDtypeStruct(shape, BF16)...  2.26 us

profile of v4, /device:TPU:1, one launch (start us, length us, event | category | flops | bytes accessed | tf_op | source)
XLA Modules:
  0.0 88.7 jit_solution(3456186269601306226)
XLA Ops:
  0.6 85.7 %shard_map.93 = (bf16[1,128,3584]{2,1,0:T(8,128)(2,1)S(1)}, bf16[4,128,256]{2,1,0:T(8,128)(2,1)S(1)}, bf16[1,3584,256]{2,1,0:T(8,128)(2,1)S(1)}, bf16[1,3584,256]{2,1,0:T(8,128)(2,1)S(1)}) custom-call(bf16[1,128,3584]{2,1,0:T(8,128)(2,1)} %tok.1, bf16[1,128,1024]{2,1,0:T(8,128)(2,1)} %cot.1, f32[4,8192]{1,0:T(4,128)} %gw.1, s32[4,64]{1,0:T(4,128)} %te.1, ...), custom_call_target="tpu_custom_call" | custom-call | tf_op jit(solution)/shard_map/pallas_call | solution.py:487
  86.3 2.3 %shard_map.94 = (bf16[1,128,3584]{2,1,0:T(8,128)(2,1)}, bf16[4,128,256]{2,1,0:T(8,128)(2,1)}, bf16[1,3584,256]{2,1,0:T(8,128)(2,1)}, bf16[1,3584,256]{2,1,0:T(8,128)(2,1)}) custom-call(bf16[1,128,3584]{2,1,0:T(8,128)(2,1)S(1)} %get-tuple-element.8.refs_0_, bf16[4,128,256]{2,1,0:T(8,128)(2,1)S(1)} %get-tuple-element.9.refs_1_, ...), custom_call_target="tpu_custom_call" | custom-call | tf_op jit(solution)/shard_map/pallas_call | solution.py:527

commit v5 on v4

--- a/solution.py
+++ b/solution.py
@@ -11,7 +11,7 @@
 F32 = jnp.float32
 BF16 = jnp.bfloat16
 K = 4
-N_COLS = 512
+N_COLS = 896
 
 
 def dot_nn(a, b):

time: 88.8 us -> 87.5 us (0.985)
  Pallas kernels: 87.9 us -> 86.6 us
    pallas_call x1, Pallas kernels: 85.7 us -> 84.3 us  [per_device(): pl.pallas_call(functools.partial(kernel, experts), out_shape=tuple((pltpu...]
where the time goes in v5:
time: 87.5 us; the launch traced here: 87.4 us
  Pallas kernels  86.6 us (99%)
    pallas_call x1, Pallas kernels, per_device(): pl.pallas_call(functools.partial(kernel, experts), out_shape=tuple((pltpu...  84.3 us
    pallas_call x1, Pallas kernels, per_device(): pl.pallas_call(store, out_shape=tuple((jax.ShapeDtypeStruct(shape, BF16)...  2.26 us

profile of v5, /device:TPU:1, one launch (start us, length us, event | category | flops | bytes accessed | tf_op | source)
XLA Modules:
  0.0 87.4 jit_solution(9757572504572500903)
XLA Ops:
  0.6 84.3 %shard_map.93 = (bf16[1,128,3584]{2,1,0:T(8,128)(2,1)S(1)}, bf16[4,128,256]{2,1,0:T(8,128)(2,1)S(1)}, bf16[1,3584,256]{2,1,0:T(8,128)(2,1)S(1)}, bf16[1,3584,256]{2,1,0:T(8,128)(2,1)S(1)}) custom-call(bf16[1,128,3584]{2,1,0:T(8,128)(2,1)} %tok.1, bf16[1,128,1024]{2,1,0:T(8,128)(2,1)} %cot.1, f32[4,8192]{1,0:T(4,128)} %gw.1, s32[4,64]{1,0:T(4,128)} %te.1, ...), custom_call_target="tpu_custom_call" | custom-call | tf_op jit(solution)/shard_map/pallas_call | solution.py:487
  85.0 2.3 %shard_map.94 = (bf16[1,128,3584]{2,1,0:T(8,128)(2,1)}, bf16[4,128,256]{2,1,0:T(8,128)(2,1)}, bf16[1,3584,256]{2,1,0:T(8,128)(2,1)}, bf16[1,3584,256]{2,1,0:T(8,128)(2,1)}) custom-call(bf16[1,128,3584]{2,1,0:T(8,128)(2,1)S(1)} %get-tuple-element.8.refs_0_, bf16[4,128,256]{2,1,0:T(8,128)(2,1)S(1)} %get-tuple-element.9.refs_1_, ...), custom_call_target="tpu_custom_call" | custom-call | tf_op jit(solution)/shard_map/pallas_call | solution.py:527
